TPU v7x, 32 devices: a whole 2x2x4 slice. The times are simulated.
32 devices in a mesh: dp: 16 (over z, y, x), tensor: 2 (over core).
Axes of the slice: x: 2, y: 2, z: 4, core: 2. Of those that a mesh axis runs over, the one named last changes fastest.
Arguments:
- current: float32 [32, 4096], P('dp'), may hold values from -6 to 6
- noise_draw: float32 [32, 4096], P('dp'), may hold values from -6 to 6
- labels: bfloat16 [32, 1152], P('dp'), may hold values from -6 to 6
- time_now: float32 [32], P('dp'), may hold values from 0.4 to 1
- step_size: float32 [32], P('dp'), may hold values from 0.005 to 0.02
- accept: int32 [32], P('dp'), may hold values 0 or 1
- patch_weight: bfloat16 [16, 1152], replicated, may hold values from -1.5 to 1.5
- time_in: bfloat16 [256, 1152], replicated, may hold values from -0.375 to 0.375
- time_out: bfloat16 [1152, 1152], replicated, may hold values from -0.1875 to 0.1875
- qkv_weight: bfloat16 [1, 1152, 3, 1152], P(None, None, None, 'tensor'), may hold values from -1 to 1
- out_weight: bfloat16 [1, 1152, 1152], P(None, None, 'tensor'), may hold values from -0.1875 to 0.1875
- ada_weight: bfloat16 [1, 1152, 3456], P(None, 'dp', 'tensor'), may hold values from -0.1875 to 0.1875
- final_ada: bfloat16 [1152, 2304], P('dp', 'tensor'), may hold values from -0.1875 to 0.1875
- final_proj: bfloat16 [1152, 16], replicated, may hold values from -0.1875 to 0.1875
Outputs:
- next_state: float32 [32, 4096], P('dp')
- error_norm: float32 [32], P('dp')
All inputs are finite; a program needn't handle non-finite values. No bound on the sum of `accept` on one device may be relied on, other than what follows from the above.
Results may differ from a plain program's by a relative error of at most 0.015.
Values may be sent and summed in bfloat16 or wider, within the bound.
No kernel may reach another device: no remote copies, remote signals or barrier semaphores. Data moves between devices by JAX's collectives and lax.ppermute only.
A program may use at most 128 MiB of HBM per device.

v0:
```python
import math

import jax
import jax.numpy as jnp
from jax import lax
from jax.sharding import PartitionSpec as P

D = 1152
PATCH_VALS = 16
HEAD_DIM = 72


beta_low = 0.1
beta_high = 20.0
tol_abs = 0.0078
tol_rel = 0.05
norm_eps = 1e-06


def beta_at(moments):
    return beta_low + (beta_high - beta_low) * moments


def sigma_at(moments):
    integral = beta_low * moments + 0.5 * (beta_high - beta_low) * moments * moments
    return jnp.sqrt(1.0 - jnp.exp(-integral))


def time_features(moments, feature_count):
    half_count = feature_count // 2
    freq_index = jnp.arange(half_count, dtype=jnp.float32)
    freq_rates = jnp.exp(-math.log(10000.0) * freq_index / half_count)
    angles = 1000.0 * moments[:, None] * freq_rates[None, :]
    return jnp.concatenate([jnp.cos(angles), jnp.sin(angles)], axis=1)


def position_table(positions, feature_count):
    half_count = feature_count // 2
    freq_index = jnp.arange(half_count, dtype=jnp.float32)
    freq_rates = jnp.exp(-math.log(10000.0) * freq_index / half_count)
    angles = positions.astype(jnp.float32)[:, None] * freq_rates[None, :]
    return jnp.concatenate([jnp.sin(angles), jnp.cos(angles)], axis=1)


def condition(moments, labels, time_in, time_out):
    features = time_features(moments, time_in.shape[0]).astype(jnp.bfloat16)
    hidden = jax.nn.silu(jnp.dot(features, time_in, preferred_element_type=jnp.float32)).astype(
        jnp.bfloat16
    )
    joined = labels.astype(jnp.float32) + jnp.dot(
        hidden, time_out, preferred_element_type=jnp.float32
    )
    return jax.nn.silu(joined).astype(jnp.bfloat16)


def layer_norm(values):
    average = jnp.mean(values, axis=-1, keepdims=True)
    centred = values - average
    spread_sq = jnp.mean(centred * centred, axis=-1, keepdims=True)
    return centred * lax.rsqrt(spread_sq + norm_eps)


def modulate(values, shift_vec, scale_vec):
    return (layer_norm(values) * (1.0 + scale_vec[:, None]) + shift_vec[:, None]).astype(
        jnp.bfloat16
    )


def drift(values, moments, noise_guess):
    beta_rate = beta_at(moments)[:, None]
    return 0.5 * beta_rate * values - beta_rate * noise_guess / sigma_at(moments)[:, None]


def attend(projected, head_dim):
    lat_count, token_count, _, feature_width = projected.shape
    head_count = feature_width // head_dim
    shaped = projected.reshape(lat_count, token_count, 3, head_count, head_dim)
    scores = jnp.einsum(
        "lqhe,lkhe->lhqk", shaped[:, :, 0], shaped[:, :, 1], preferred_element_type=jnp.float32
    ) * head_dim ** (-0.5)
    attn_probs = jax.nn.softmax(scores, axis=-1).astype(jnp.bfloat16)
    mixture = jnp.einsum(
        "lhqk,lkhe->lqhe", attn_probs, shaped[:, :, 2], preferred_element_type=jnp.float32
    )
    return mixture.astype(jnp.bfloat16).reshape(lat_count, token_count, feature_width)


def shards(
    current,
    noise_draw,
    labels,
    time_now,
    step_size,
    accept,
    patch_weight,
    time_in,
    time_out,
    qkv_weight,
    out_weight,
    ada_weight,
    final_ada,
    final_proj,
):
    lat_count = current.shape[0]
    tok_count = current.shape[1] // PATCH_VALS
    layer_total = ada_weight.shape[0]
    layer_cols = ada_weight.shape[2]
    final_cols = final_ada.shape[1]
    tensor_size = lax.axis_size("tensor")
    later_time = time_now - step_size
    moments = jnp.concatenate([time_now, later_time])
    cond_act = condition(moments, jnp.concatenate([labels, labels], axis=0), time_in, time_out)
    own_rows = ada_weight.shape[1]
    packed = jnp.concatenate(
        [ada_weight.transpose(1, 0, 2).reshape(own_rows, layer_total * layer_cols), final_ada],
        axis=1,
    )
    row_total = cond_act.shape[0]
    packed_width = packed.shape[1]
    mod_local = jnp.dot(
        cond_act,
        lax.all_gather(packed, "dp", axis=0, tiled=True),
        preferred_element_type=jnp.float32,
    )
    gathered = lax.all_gather(mod_local.astype(jnp.bfloat16), "tensor", axis=1, tiled=True).astype(
        mod_local.dtype
    )
    arranged = gathered.reshape(row_total, tensor_size, packed_width)
    layer_mods = arranged[:, :, : layer_total * layer_cols].reshape(
        row_total, tensor_size, layer_total, layer_cols
    )
    layer_mods = layer_mods.transpose(0, 2, 1, 3).reshape(
        row_total, layer_total, tensor_size * layer_cols
    )
    final_mods = arranged[:, :, layer_total * layer_cols :].reshape(
        row_total, tensor_size * final_cols
    )
    positions = position_table(jnp.arange(tok_count, dtype=jnp.int32), D)

    def evaluate(latents, mod_rows, final_rows):
        tokens = latents.reshape(lat_count, tok_count, PATCH_VALS).astype(jnp.bfloat16)
        stream = (
            jnp.einsum("ltc,cd->ltd", tokens, patch_weight, preferred_element_type=jnp.float32)
            + positions[None]
        )
        shift_attn, scale_attn, gate_attn = jnp.split(mod_rows[:, 0], 3, axis=1)
        attn_in = modulate(stream, shift_attn, scale_attn)
        projected = jnp.einsum(
            "ltd,dck->ltck", attn_in, qkv_weight[0], preferred_element_type=jnp.float32
        ).astype(jnp.bfloat16)
        attended = attend(projected, HEAD_DIM)
        partial_value = jnp.einsum(
            "ltk,dk->ltd", attended, out_weight[0], preferred_element_type=jnp.float32
        )
        attn_sum = lax.psum(partial_value.astype(jnp.bfloat16), "tensor").astype(jnp.float32)
        stream = stream + gate_attn[:, None] * attn_sum
        shift_final, scale_final = jnp.split(final_rows, 2, axis=1)
        final_in = modulate(stream, shift_final, scale_final)
        guessed = jnp.einsum(
            "ltd,dc->ltc", final_in, final_proj, preferred_element_type=jnp.float32
        )
        return guessed.reshape(lat_count, tok_count * PATCH_VALS)

    noise_now = evaluate(current, layer_mods[:lat_count], final_mods[:lat_count])
    drift_now = drift(current, time_now, noise_now)
    spread = jnp.sqrt(step_size * beta_at(time_now))[:, None] * noise_draw
    euler_state = current + step_size[:, None] * drift_now + spread
    noise_later = evaluate(euler_state, layer_mods[lat_count:], final_mods[lat_count:])
    drift_later = drift(euler_state, later_time, noise_later)
    heun_state = current + 0.5 * step_size[:, None] * (drift_now + drift_later) + spread
    scale_ref = jnp.maximum(tol_abs, tol_rel * jnp.maximum(jnp.abs(heun_state), jnp.abs(current)))
    scaled_gap = (euler_state - heun_state) / scale_ref
    error_norm = jnp.sqrt(jnp.sum(scaled_gap * scaled_gap, axis=1) / current.shape[1])
    next_state = jnp.where(accept[:, None] == 1, heun_state, current)
    return (next_state, error_norm)


def solution(mesh):
    in_specs = (
        P("dp", None),
        P("dp", None),
        P("dp", None),
        P("dp"),
        P("dp"),
        P("dp"),
        P(),
        P(),
        P(),
        P(None, None, None, "tensor"),
        P(None, None, "tensor"),
        P(None, "dp", "tensor"),
        P("dp", "tensor"),
        P(),
    )
    out_specs = (P("dp", None), P("dp"))
    return jax.shard_map(shards, mesh=mesh, in_specs=in_specs, out_specs=out_specs, check_vma=False)
```

profile of v0, /device:TPU:0, one launch (start us, length us, event | category | flops | bytes accessed | tf_op | source)
XLA Modules:
  0.0 200.8 jit_solution(1456404934504818593)
XLA Ops:
  7.2 2.1 %pad_maximum_fusion.1 = bf16[72,2880]{1,0:T(8,128)(2,1)} fusion(bf16[72,1152]{1,0:T(8,128)(2,1)} %param.26, bf16[72,1728]{1,0:T(8,128)(2,1)} %bitcast.104), kind=kLoop, calls=%fused_computation.66 | loop fusion | flops 829440 | bytes 829440 | tf_op jit(solution)/shard_map/concatenate | solution.py:114
  9.4 0.8 convert_element_type.83
  11.8 2.4 %multiply_sine_fusion = (f32[256,576]{1,0:T(8,128)S(1)}, f32[256,576]{1,0:T(8,128)S(1)}) fusion(f32[576]{0:T(1024)S(1)} %multiply_exponential_fusion, f32[256]{0:T(256)S(1)} %iota_convert_fusion), kind=kLoop, calls=%fused_computation.55 | loop fusion | flops 147456 | bytes 1182976 | tf_op jit(solution)/shard_map/sin | solution.py:42
  14.4 1.0 copy-done.5
  15.9 1.4 copy-done.1
  18.1 93.2 %all-gather.3.cloned.1.call-done = bf16[1152,2880]{1,0:T(8,128)(2,1)} async-done(((bf16[72,2880]{1,0:T(8,128)(2,1)}), bf16[1152,2880]{1,0:T(8,128)(2,1)}) %all-gather.3.cloned.1.call-update) | async-done | bytes 6635536 | tf_op jit(solution)/shard_map/all_gather | solution.py:122
  111.3 4.3 %fusion.8 = bf16[1,2880,4]{1,2,0:T(4,128)(2,1)S(1)} fusion(bf16[1152,2880]{1,0:T(8,128)(2,1)} %all-gather.3.cloned.1.call-done, bf16[1152,1152]{1,0:T(8,128)(2,1)S(1)} %copy-done, f32[4,1152]{1,0:T(4,128)S(1)} %fusion.62, bf16[2,1152]{1,0:T(2,128)(2,1)S(1)} %copy-done.12), kind=kOutput, calls=%fused_computation.17 | convolution fusion | flops 37239552 | bytes 9335808 | tf_op jit(solution)/shard_map/dot_general | solution.py:120
  115.6 1.8 all-gather
  118.0 5.6 %fusion.17 = bf16[2,256,3,576]{1,3,2,0:T(8,128)(2,1)S(1)} fusion(bf16[1,1152,3,576]{1,3,2,0:T(8,128)(2,1)} %param.23, f32[2,256,1152]{2,1,0:T(8,128)} %copy-done.1, f32[2,1152]{1,0:T(2,128)S(1)} %get-tuple-element.17, f32[2,1152]{1,0:T(2,128)S(1)} %get-tuple-element.18, f32[2,256]{1,0:T(2,128)S(1)} %add_rsqrt_fusion.3, ...), kind=kOutput, calls=%fused_computation.35 | convolution fusion | flops 2042265600 | bytes 8132608 | tf_op jit(solution)/shard_map/ltd,dck->ltck/dot_general | solution.py:148
  124.3 3.2 %fusion.79 = (f32[2,8,256]{2,1,0:T(8,128)S(1)}, f32[2,8,256,256]{2,3,1,0:T(8,128)S(1)}) fusion(f32[2,8,256,256]{2,3,1,0:T(8,128)S(1)} %fusion.44), kind=kOutput, calls=%fused_computation.137 | output fusion | flops 4194559 | bytes 8404992 | tf_op jit(solution)/shard_map/sub | solution.py:81
  128.1 0.8 copy-done.15
  128.9 2.2 %convolution_convert_fusion.2 = bf16[2,256,1152]{2,1,0:T(8,128)(2,1)} fusion(bf16[2,256,576]{1,2,0:T(8,128)(2,1)S(1)} %bitcast.107, bf16[1,1152,576]{1,2,0:T(8,128)(2,1)S(1)} %copy-done.15), kind=kOutput, calls=%fused_computation.19 | convolution fusion | flops 680067072 | bytes 3096576 | tf_op jit(solution)/shard_map/ltk,dk->ltd/dot_general | solution.py:152
  131.5 17.9 %all-reduce.3.cloned.1.call-done = bf16[2,256,1152]{2,1,0:T(8,128)(2,1)} async-done(((bf16[2,256,1152]{2,1,0:T(8,128)(2,1)}), bf16[2,256,1152]{2,1,0:T(8,128)(2,1)}) %all-reduce.3.cloned.1.call-update) | async-done | bytes 1179664 | tf_op jit(solution)/shard_map/psum | solution.py:155
  149.4 2.5 %fusion.41 = f32[2,256]{1,0:T(2,128)S(1)} fusion(f32[2,256,1152]{2,1,0:T(8,128)} %copy-done.1, bf16[2,256,1152]{2,1,0:T(8,128)(2,1)} %all-reduce.3.cloned.1.call-done, f32[2,1152]{1,0:T(2,128)S(1)} %get-tuple-element.16), kind=kLoop, calls=%fused_computation.56 | loop fusion | flops 2358784 | bytes 3550208 | tf_op jit(solution)/shard_map/reduce_sum | solution.py:57
  153.1 0.8 fusion.39
  154.4 1.9 fusion.80
  156.8 2.8 %fusion.20 = bf16[2,256,3,576]{1,3,2,0:T(8,128)(2,1)S(1)} fusion(bf16[1,1152,3,576]{1,3,2,0:T(8,128)(2,1)S(1)} %copy-done.14, f32[2,256,1152]{2,1,0:T(8,128)S(1)} %get-tuple-element.39, f32[2,1152]{1,0:T(2,128)S(1)} %get-tuple-element.14, f32[2,1152]{1,0:T(2,128)S(1)} %get-tuple-element.15, f32[2,256]{1,0:T(2,128)S(1)} %add_rsqrt_fusion.1, ...), kind=kOutput, calls=%fused_computation.36 | convolution fusion | flops 2042265600 | bytes 8132608 | tf_op jit(solution)/shard_map/ltd,dck->ltck/dot_general | solution.py:148
  159.6 0.8 fusion.43
  160.4 3.2 %fusion.81 = (f32[2,8,256]{2,1,0:T(8,128)S(1)}, f32[2,8,256,256]{2,3,1,0:T(8,128)S(1)}) fusion(f32[2,8,256,256]{2,3,1,0:T(8,128)S(1)} %fusion.43), kind=kOutput, calls=%fused_computation.139 | output fusion | flops 4194559 | bytes 8404992 | tf_op jit(solution)/shard_map/sub | solution.py:81
  164.1 0.8 copy-done.16
  164.9 2.2 %convolution_convert_fusion.1 = bf16[2,256,1152]{2,1,0:T(8,128)(2,1)} fusion(bf16[2,256,576]{1,2,0:T(8,128)(2,1)S(1)} %bitcast.108, bf16[1,1152,576]{1,2,0:T(8,128)(2,1)S(1)} %copy-done.16), kind=kOutput, calls=%fused_computation.18 | convolution fusion | flops 680067072 | bytes 3096576 | tf_op jit(solution)/shard_map/ltk,dk->ltd/dot_general | solution.py:152
  167.2 20.9 %all-reduce.5.cloned.1.call-done = bf16[2,256,1152]{2,1,0:T(8,128)(2,1)} async-done(((bf16[2,256,1152]{2,1,0:T(8,128)(2,1)}), bf16[2,256,1152]{2,1,0:T(8,128)(2,1)}) %all-reduce.5.cloned.1.call-update) | async-done | bytes 1179664 | tf_op jit(solution)/shard_map/psum | solution.py:155
  188.2 2.5 %fusion.42 = f32[2,256]{1,0:T(2,128)S(1)} fusion(f32[2,256,1152]{2,1,0:T(8,128)} %copy-done.3, bf16[2,256,1152]{2,1,0:T(8,128)(2,1)} %all-reduce.5.cloned.1.call-done, f32[2,1152]{1,0:T(2,128)S(1)} %get-tuple-element.13), kind=kLoop, calls=%fused_computation.57 | loop fusion | flops 2358784 | bytes 3550208 | tf_op jit(solution)/shard_map/reduce_sum | solution.py:57
  191.8 0.8 fusion.40
  (87 shorter events, 10.7 us)
Async XLA Ops:
  7.2 104.1 %copy-start = (bf16[1152,1152]{1,0:T(8,128)(2,1)S(1)}, bf16[1152,1152]{1,0:T(8,128)(2,1)}, u32[]{:S(2)}) copy-start(bf16[1152,1152]{1,0:T(8,128)(2,1)} %param.22) | copy-start | bytes 7962628
  7.2 104.1 %all-gather.3.cloned.1.call-start = ((), (), s32[]{:S(2)}) async-start(), calls=%async_computation | async-start | bytes 7206912 | tf_op jit(solution)/shard_map/all_gather | solution.py:122
  9.3 6.1 %copy-start.10 = (bf16[16,1152]{1,0:T(8,128)(2,1)S(1)}, bf16[16,1152]{1,0:T(8,128)(2,1)}, u32[]{:S(2)}) copy-start(bf16[16,1152]{1,0:T(8,128)(2,1)} %param.20) | copy-start | bytes 110596
  9.3 140.1 %all-reduce.3.cloned.1.call-start = ((), (), s32[]{:S(2)}) async-start(), calls=%async_computation.1 | async-start | bytes 2359296 | tf_op jit(solution)/shard_map/psum | solution.py:155
  14.4 1.0 copy-start.5
  15.4 2.5 %copy-start.8 = (bf16[256,1152]{1,0:T(8,128)(2,1)S(1)}, bf16[256,1152]{1,0:T(8,128)(2,1)}, u32[]{:S(2)}) copy-start(bf16[256,1152]{1,0:T(8,128)(2,1)} %param.21) | copy-start | bytes 1769476
  15.9 1.5 copy-start.1
  15.9 95.4 %copy-start.12 = (bf16[2,1152]{1,0:T(2,128)(2,1)S(1)}, bf16[2,1152]{1,0:T(2,128)(2,1)}, u32[]{:S(2)}) copy-start(bf16[2,1152]{1,0:T(2,128)(2,1)} %param.16) | copy-start | bytes 13828
  127.6 1.3 copy-start.15
  131.2 57.0 %all-reduce.5.cloned.1.call-start = ((), (), s32[]{:S(2)}) async-start(), calls=%async_computation.2 | async-start | bytes 2359296 | tf_op jit(solution)/shard_map/psum | solution.py:155
  149.4 2.7 %copy-start.2 = (f32[2,256,1152]{2,1,0:T(8,128)S(1)}, f32[2,256,1152]{2,1,0:T(8,128)}, u32[]{:S(2)}) copy-start(f32[2,256,1152]{2,1,0:T(8,128)} %copy-done.1) | copy-start | bytes 7077892
  149.4 3.0 %copy-start.6 = (bf16[2,256,1152]{2,1,0:T(8,128)(2,1)S(1)}, bf16[2,256,1152]{2,1,0:T(8,128)(2,1)}, u32[]{:S(2)}) copy-start(bf16[2,256,1152]{2,1,0:T(8,128)(2,1)} %all-reduce.3.cloned.1.call-done) | copy-start | bytes 3538948
  152.0 1.1 copy-start.17
  153.0 1.0 copy-start.9
  153.1 1.0 copy-start.11
  153.1 1.0 copy-start.13
  154.3 2.5 %copy-start.14 = (bf16[1,1152,3,576]{1,3,2,0:T(8,128)(2,1)S(1)}, bf16[1,1152,3,576]{1,3,2,0:T(8,128)(2,1)}, u32[]{:S(2)}) copy-start(bf16[1,1152,3,576]{1,3,2,0:T(8,128)(2,1)} %param.23) | copy-start | bytes 11943940
  156.3 3.3 %copy-start.3 = (f32[2,256,1152]{2,1,0:T(8,128)}, f32[2,256,1152]{2,1,0:T(8,128)S(1)}, u32[]{:S(2)}) copy-start(f32[2,256,1152]{2,1,0:T(8,128)S(1)} %get-tuple-element.39) | copy-start | bytes 7077892
  163.6 1.3 copy-start.16
  164.9 2.2 %copy-start.18 = (s32[2]{0:T(128)S(1)}, s32[2]{0:T(128)}, u32[]{:S(2)}) copy-start(s32[2]{0:T(128)} %param.19) | copy-start | bytes 28
  188.2 2.7 %copy-start.4 = (f32[2,256,1152]{2,1,0:T(8,128)S(1)}, f32[2,256,1152]{2,1,0:T(8,128)}, u32[]{:S(2)}) copy-start(f32[2,256,1152]{2,1,0:T(8,128)} %copy-done.3) | copy-start | bytes 7077892
  188.2 3.0 %copy-start.7 = (bf16[2,256,1152]{2,1,0:T(8,128)(2,1)S(1)}, bf16[2,256,1152]{2,1,0:T(8,128)(2,1)}, u32[]{:S(2)}) copy-start(bf16[2,256,1152]{2,1,0:T(8,128)(2,1)} %all-reduce.5.cloned.1.call-done) | copy-start | bytes 3538948
Sparse Core Ops, SparseCore 0:
  10.7 100.5 all-gather.2
  131.3 18.1 all-reduce.2
  167.3 20.8 all-reduce.4
where the time goes:
time: 201 us
  waiting for transfers between devices  132 us (66%)
  matrix products  23.8 us (12%)
  other arithmetic  22.1 us (11%)
  between operations  14.1 us (7%)
  local copies, waits for them, and re-layouts  6.5 us (3%)
    all_gather x1, waiting for transfers between devices, shards(): lax.all_gather(packed, 'dp', axis=0, tiled=True)  93.2 us
    psum x2, waiting for transfers between devices, evaluate(): lax.psum(partial_value.astype(jnp.bfloat16), 'tensor').astype(jnp.float32)  38.8 us
    dot_general x2, matrix products, evaluate(): jnp.einsum('ltd,dck->ltck', attn_in, qkv_weight[0], preferred_element_typ...  8.31 us
    sub x2, other arithmetic, attend(): attn_probs = jax.nn.softmax(scores, axis=-1).astype(jnp.bfloat16)  6.48 us
    unnamed x41, local copies, waits for them, and re-layouts  5.37 us
    reduce_sum x2, other arithmetic, layer_norm(): average = jnp.mean(values, axis=-1, keepdims=True)  5.04 us
    dot_general x2, matrix products, evaluate(): jnp.einsum('ltk,dk->ltd', attended, out_weight[0], preferred_element_type...  4.45 us
    dot_general x1, matrix products, shards(): jnp.dot(cond_act, lax.all_gather(packed, 'dp', axis=0, tiled=True), prefe...  4.3 us
  transfers between devices with their start and end apart: 3, of which 3 were waited for; matrix products, arithmetic and copies ran while one was open for 3% of the time, Pallas kernels for 0%

commit v1 on v0

v1 whole, which is shorter than its diff:
```python
import functools
import math

import jax
import jax.numpy as jnp
import numpy as np
from jax import lax
from jax.experimental import pallas as pl
from jax.experimental.pallas import tpu as pltpu
from jax.sharding import PartitionSpec as P

HEAD_DIM = 72
LANES = 128
ROWS = 8

beta_low = 0.1
beta_high = 20.0
tol_abs = 0.0078
tol_rel = 0.05
norm_eps = 1e-06

f32 = jnp.float32
bf16 = jnp.bfloat16
VM = pl.BlockSpec(memory_space=pltpu.VMEM)
SM = pl.BlockSpec(memory_space=pltpu.SMEM)


def up(size, unit):
    return -(-size // unit) * unit


def mm(a, b):
    return lax.dot_general(a, b, (((1,), (0,)), ((), ())), preferred_element_type=f32)


def mm_t(a, b):
    return lax.dot_general(a, b, (((1,), (1,)), ((), ())), preferred_element_type=f32)


def silu(v):
    return v / (1.0 + jnp.exp(-v))


def position_table(token_count, width):
    half = width // 2
    rates = np.exp(-math.log(10000.0) * np.arange(half) / half)
    angles = np.arange(token_count)[:, None] * rates[None, :]
    return np.concatenate([np.sin(angles), np.cos(angles)], axis=1).astype(np.float32)


def tell_kernel(core_ref, time_ref, step_ref, labels_ref, out_ref, block):
    mine = core_ref[0]
    tiles = labels_ref.shape[1] // LANES
    both = labels_ref[...].astype(f32)
    row = jnp.where(mine == 0, both[0:1], both[1:2])
    block[...] = jnp.zeros_like(block)
    for tile in range(tiles):
        block[tile : tile + 1, :] = row[:, tile * LANES : (tile + 1) * LANES]
    now = time_ref[mine]
    later = now - step_ref[mine]
    block[tiles : tiles + 1, :] = jnp.full((1, LANES), now, f32)
    block[tiles + 1 : tiles + 2, :] = jnp.full((1, LANES), later, f32)
    for dest in range(out_ref.shape[0]):
        out_ref[dest] = block[...]


def part_kernel(
    place_ref, heard_ref, rates_ref, time_in_ref, time_out_ref,
    ada_own, ada_other, fin_own, fin_other, out_ref, part,
):
    count = heard_ref.shape[0]
    width = time_out_ref.shape[0]
    tiles = width // LANES
    own_rows = ada_own.shape[0]
    labels = jnp.concatenate([heard_ref[:, tile, :] for tile in range(tiles)], axis=1)
    labels = jnp.concatenate([labels, labels], axis=0)
    moments = jnp.concatenate([heard_ref[:, tiles, :], heard_ref[:, tiles + 1, :]], axis=0)
    angles = 1000.0 * moments * rates_ref[...]
    features = jnp.concatenate([jnp.cos(angles), jnp.sin(angles)], axis=1).astype(bf16)
    hidden = silu(mm(features, time_in_ref[...])).astype(bf16)
    cond = silu(labels + mm(hidden, time_out_ref[...])).astype(bf16)
    first = place_ref[1] * own_rows
    pick_shape = (width, LANES)
    pick = lax.broadcasted_iota(jnp.int32, pick_shape, 0) == (
        lax.broadcasted_iota(jnp.int32, pick_shape, 1) + first
    )
    own_cond = mm(cond, pick.astype(f32).astype(bf16))[:, :own_rows].astype(bf16)
    low = place_ref[0] == 0
    wide = up(ada_own.shape[1], LANES)
    for at, own, other in ((0, ada_own, ada_other), (2 * wide, fin_own, fin_other)):
        a = mm(own_cond, own[...])
        b = mm(own_cond, other[...])
        used = a.shape[1]
        gap = up(used, LANES)
        part[:, at : at + used] = jnp.where(low, a, b)
        part[:, at + gap : at + gap + used] = jnp.where(low, b, a)
        if gap != used:
            part[:, at + used : at + gap] = jnp.zeros((2 * count, gap - used), f32)
            part[:, at + gap + used : at + 2 * gap] = jnp.zeros((2 * count, gap - used), f32)
    for dest in range(count):
        now_row = part[dest : dest + 1, :]
        later_row = part[count + dest : count + dest + 1, :]
        out_ref[dest] = jnp.concatenate([now_row, later_row], axis=0).astype(bf16)


def norm(v):
    width = v.shape[1]
    average = jnp.sum(v, axis=1, keepdims=True) * (1.0 / width)
    centred = v - average
    spread_sq = jnp.sum(centred * centred, axis=1, keepdims=True) * (1.0 / width)
    return centred * lax.rsqrt(spread_sq + norm_eps)


def step_kernel(
    core_ref, time_ref, step_ref, accept_ref, cur_ref, noise_ref, pos_ref, patch_ref,
    qkv_own, qkv_other, out_own, out_other, proj_ref, mods_ref, out_ref,
    cur32, nse32, state32, guess32, modv, patch8, proj8, stream, inner, qkv, mixed,
):
    mine = core_ref[0]
    low_core = mine == 0
    lat_rows = cur32.shape[0]
    tokens, width = stream.shape
    half = qkv_own.shape[2]
    padded = qkv.shape[3]
    heads = half // HEAD_DIM
    count = mods_ref.shape[0]
    vals = patch_ref.shape[0]
    reps = LANES // vals

    for row in range(lat_rows):
        lanes = slice(row * LANES, (row + 1) * LANES)
        cur32[row : row + 1, :] = jnp.where(low_core, cur_ref[0:1, lanes], cur_ref[1:2, lanes])
        nse32[row : row + 1, :] = jnp.where(low_core, noise_ref[0:1, lanes], noise_ref[1:2, lanes])
    for rep in range(reps):
        patch8[rep * vals : (rep + 1) * vals, :] = patch_ref[...]
        proj8[rep * vals : (rep + 1) * vals, :] = proj_ref[...]
    if padded != half:
        qkv[:, :, :, half:] = jnp.zeros(qkv.shape[:3] + (padded - half,), bf16)

    total = mods_ref[0].astype(f32)
    for source in range(1, count):
        total = total + mods_ref[source].astype(f32)
    lay_cols = 3 * width // 2
    wide = up(lay_cols, LANES)
    low = total[:, :wide]
    high = total[:, wide : 2 * wide]
    lane = lax.broadcasted_iota(jnp.int32, (2, width), 1)
    rest = low[:, width:]
    rest = jnp.concatenate([rest, jnp.zeros((2, width - rest.shape[1]), f32)], axis=1)
    split = lay_cols - width
    scale_attn = jnp.where(lane < split, rest, pltpu.roll(high[:, :width], split, 1))
    gate_attn = pltpu.roll(high, wide - (width - split), 1)[:, :width]
    for moment in range(2):
        row = slice(moment, moment + 1)
        modv[moment, 0:1, :] = low[row, :width]
        modv[moment, 1:2, :] = 1.0 + scale_attn[row]
        modv[moment, 2:3, :] = gate_attn[row]
        modv[moment, 3:4, :] = total[row, 2 * wide : 2 * wide + width]
        modv[moment, 4:5, :] = 1.0 + total[row, 2 * wide + width : 2 * wide + 2 * width]

    now = jnp.full((1, LANES), time_ref[mine], f32)
    step = jnp.full((1, LANES), step_ref[mine], f32)
    later = now - step

    def beta_at(m):
        return beta_low + (beta_high - beta_low) * m

    def drift(values, m, guess):
        rate = beta_at(m)
        integral = beta_low * m + 0.5 * (beta_high - beta_low) * m * m
        return 0.5 * rate * values - rate * guess / jnp.sqrt(1.0 - jnp.exp(-integral))

    spread = jnp.sqrt(step * beta_at(now)) * nse32[...]
    group = lax.broadcasted_iota(jnp.int32, (tokens, LANES), 1) // vals
    own_slot = group == lax.broadcasted_iota(jnp.int32, (tokens, LANES), 0) % reps
    exp_scale = HEAD_DIM**-0.5 * math.log2(math.e)

    def evaluate(index, carry):
        del carry
        x = state32[...]
        tok = jnp.broadcast_to(x[:, None, :], (lat_rows, reps, LANES)).reshape(tokens, LANES)
        tok = jnp.where(own_slot, tok, 0.0).astype(bf16)
        stream[...] = mm(tok, patch8[...]) + pos_ref[...]
        inner[...] = (norm(stream[...]) * modv[index, 1:2, :] + modv[index, 0:1, :]).astype(bf16)
        for part, weight in enumerate((qkv_own, qkv_other)):
            for kind in range(3):
                qkv[part, kind, :, :half] = mm(inner[...], weight[kind]).astype(bf16)
        for part in range(2):
            mixed[...] = jnp.zeros_like(mixed)
            for head in range(heads):
                begin = head * HEAD_DIM
                lo = begin // LANES * LANES
                hi = up(begin + HEAD_DIM, LANES)
                at = lax.broadcasted_iota(jnp.int32, (tokens, hi - lo), 1) + lo
                inside = (at >= begin) & (at < begin + HEAD_DIM)
                q = jnp.where(inside, qkv[part, 0, :, lo:hi], jnp.zeros((), bf16))
                v = jnp.where(inside, qkv[part, 2, :, lo:hi], jnp.zeros((), bf16))
                scores = mm_t(q, qkv[part, 1, :, lo:hi])
                top = jnp.max(scores, axis=1, keepdims=True)
                probs = jnp.exp2((scores - top) * exp_scale)
                scale = 1.0 / jnp.sum(probs, axis=1, keepdims=True)
                mixed[:, lo:hi] += mm(probs.astype(bf16), v) * scale
            weight = (out_own, out_other)[part]
            value = mm(mixed[:, :half].astype(bf16), weight[...])
            stream[...] += modv[index, 2:3, :] * value
        inner[...] = (norm(stream[...]) * modv[index, 4:5, :] + modv[index, 3:4, :]).astype(bf16)
        guess = jnp.where(own_slot, mm_t(inner[...], proj8[...]), 0.0)
        guess = jnp.sum(guess.reshape(lat_rows, reps, LANES), axis=1)
        guess32[index] = guess

        @pl.when(index == 0)
        def _():
            state32[...] = cur32[...] + step * drift(cur32[...], now, guess) + spread

        return 0

    state32[...] = cur32[...]
    lax.fori_loop(0, 2, evaluate, 0)

    cur = cur32[...]
    euler = state32[...]
    drift_now = drift(cur, now, guess32[0])
    drift_later = drift(euler, later, guess32[1])
    heun = cur + 0.5 * step * (drift_now + drift_later) + spread
    scale_ref = jnp.maximum(tol_abs, tol_rel * jnp.maximum(jnp.abs(heun), jnp.abs(cur)))
    gap = (euler - heun) / scale_ref
    square = jnp.sum(jnp.sum(gap * gap, axis=1, keepdims=True), axis=0, keepdims=True)
    error = jnp.sqrt(square / (lat_rows * LANES))
    out_ref[:lat_rows, :] = jnp.where(accept_ref[mine] == 1, heun, cur)
    out_ref[lat_rows:, :] = jnp.broadcast_to(error, (ROWS, LANES))


def shards(
    current, noise_draw, labels, time_now, step_size, accept, patch_weight, time_in,
    time_out, qkv_weight, out_weight, ada_weight, final_ada, final_proj,
):
    count = lax.axis_size("dp")
    width = time_out.shape[0]
    latent = current.shape[1]
    vals = patch_weight.shape[0]
    tokens = latent // vals
    half = qkv_weight.shape[3]
    core = lax.axis_index("tensor").astype(jnp.int32)
    place = jnp.stack([core, lax.axis_index("dp").astype(jnp.int32)])
    swap = functools.partial(lax.ppermute, axis_name="tensor", perm=[(0, 1), (1, 0)])

    qkv = qkv_weight[0].transpose(1, 0, 2)
    out = out_weight[0].T
    ada = ada_weight[0]

    ada_other, fin_other = swap(ada), swap(final_ada)
    qkv_other, out_other = swap(qkv), swap(out)

    tell_rows = up(width // LANES + 2, ROWS)
    told = pl.pallas_call(
        tell_kernel,
        out_shape=jax.ShapeDtypeStruct((count, tell_rows, LANES), f32),
        in_specs=[SM, SM, SM, VM],
        out_specs=VM,
        scratch_shapes=[pltpu.VMEM((tell_rows, LANES), f32)],
        compiler_params=pltpu.CompilerParams(vmem_limit_bytes=4 << 20),
    )(place, time_now, step_size, labels)
    heard = lax.all_to_all(told, "dp", 0, 0, tiled=True)

    half_freq = time_in.shape[0] // 2
    rates = np.exp(-math.log(10000.0) * np.arange(half_freq) / half_freq)
    rates = jnp.asarray(rates.astype(np.float32)[None])
    cols = 2 * up(ada.shape[1], LANES) + 2 * final_ada.shape[1]
    parts = pl.pallas_call(
        part_kernel,
        out_shape=jax.ShapeDtypeStruct((count, 2, cols), bf16),
        in_specs=[SM] + [VM] * 8,
        out_specs=VM,
        scratch_shapes=[pltpu.VMEM((2 * count, cols), f32)],
        compiler_params=pltpu.CompilerParams(vmem_limit_bytes=16 << 20),
    )(place, heard, rates, time_in, time_out, ada, ada_other, final_ada, fin_other)
    mods = lax.all_to_all(parts, "dp", 0, 0, tiled=True)

    lat_rows = latent // LANES
    padded = up(half, LANES)
    positions = jnp.asarray(position_table(tokens, width))
    small = pltpu.VMEM((lat_rows, LANES), f32)
    done = pl.pallas_call(
        step_kernel,
        out_shape=jax.ShapeDtypeStruct((lat_rows + ROWS, LANES), f32),
        in_specs=[SM] * 4 + [VM] * 10,
        out_specs=VM,
        scratch_shapes=[
            small, small, small,
            pltpu.VMEM((2, lat_rows, LANES), f32),
            pltpu.VMEM((2, ROWS, width), f32),
            pltpu.VMEM((LANES, width), bf16),
            pltpu.VMEM((LANES, width), bf16),
            pltpu.VMEM((tokens, width), f32),
            pltpu.VMEM((tokens, width), bf16),
            pltpu.VMEM((2, 3, tokens, padded), bf16),
            pltpu.VMEM((tokens, padded), f32),
        ],
        compiler_params=pltpu.CompilerParams(vmem_limit_bytes=40 << 20),
    )(
        place, time_now, step_size, accept, current, noise_draw, positions, patch_weight,
        qkv, qkv_other, out, out_other, final_proj.T, mods,
    )
    other = swap(done)
    first = jnp.where(core == 0, done, other)
    second = jnp.where(core == 0, other, done)
    both = jnp.stack([first, second])
    next_state = both[:, :lat_rows].reshape(2, latent)
    return (next_state, both[:, lat_rows, 0])


def solution(mesh):
    in_specs = (
        P("dp", None),
        P("dp", None),
        P("dp", None),
        P("dp"),
        P("dp"),
        P("dp"),
        P(),
        P(),
        P(),
        P(None, None, None, "tensor"),
        P(None, None, "tensor"),
        P(None, "dp", "tensor"),
        P("dp", "tensor"),
        P(),
    )
    out_specs = (P("dp", None), P("dp"))
    return jax.shard_map(shards, mesh=mesh, in_specs=in_specs, out_specs=out_specs, check_vma=False)
```

time: 201 us -> 70.3 us (0.35)
  waiting for transfers between devices: 132 us -> 9 us
  matrix products: 23.8 us -> 0 us
  other arithmetic: 22.1 us -> 0.7 us
  local copies, waits for them, and re-layouts: 6.5 us -> 27.1 us
  Pallas kernels: 0 us -> 19.1 us
  between operations: 14.1 us -> 0.8 us
  starting transfers between devices: 0.3 us -> 12.8 us
    all_gather x1 -> x0, waiting for transfers between devices: 93.2 us -> none  [shards(): lax.all_gather(packed, 'dp', axis=0, tiled=True)]
    psum x2 -> x0, waiting for transfers between devices: 38.8 us -> none  [evaluate(): lax.psum(partial_value.astype(jnp.bfloat16), 'tensor').astype(jnp.float32)]
    dot_general x14 -> x0, matrix products: 23.8 us -> none  [the longest x2 8.31 us: evaluate(): jnp.einsum('ltd,dck->ltck', attn_in, qkv_weight[0], preferred_element_typ...]
    pallas_call x0 -> x3, Pallas kernels: none -> 19.1 us  [the longest x1 14.9 us: shards(): pl.pallas_call(step_kernel, out_shape=jax.ShapeDtypeStruct((lat_rows + RO...]
    unnamed x41 -> x40, local copies, waits for them, and re-layouts: 5.37 us -> 20.4 us
    all_to_all x0 -> x2, starting transfers between devices: none -> 11.5 us  [the longest x1 7.93 us: shards(): heard = lax.all_to_all(told, 'dp', 0, 0, tiled=True)]
    reduce_sum x7 -> x0, other arithmetic: 7.18 us -> none  [the longest x2 5.04 us: layer_norm(): average = jnp.mean(values, axis=-1, keepdims=True)]
    ppermute x0 -> x1, local copies, waits for them, and re-layouts: none -> 6.7 us  [shards(): qkv_other, out_other = (swap(qkv), swap(out))]
  transfers between devices with their start and end apart: 3 -> 7, of which waited for: 3 -> 3; matrix products, arithmetic and copies ran while one was open for 3% -> 19% of each run, Pallas kernels for 0% -> 6%
where the time goes in v1:
time: 70.3 us; the launch traced here: 69.5 us
  local copies, waits for them, and re-layouts  27.1 us (39%)
  Pallas kernels  19.1 us (27%)
  starting transfers between devices  12.8 us (18%)
  waiting for transfers between devices  9 us (13%)
  between operations  0.8 us (1%)
    unnamed x40, local copies, waits for them, and re-layouts  20.4 us
    pallas_call x1, Pallas kernels, shards(): pl.pallas_call(step_kernel, out_shape=jax.ShapeDtypeStruct((lat_rows + RO...  14.9 us
    all_to_all x1, starting transfers between devices, shards(): heard = lax.all_to_all(told, 'dp', 0, 0, tiled=True)  7.93 us
    ppermute x1, local copies, waits for them, and re-layouts, shards(): qkv_other, out_other = (swap(qkv), swap(out))  6.7 us
    all_to_all x1, waiting for transfers between devices, shards(): heard = lax.all_to_all(told, 'dp', 0, 0, tiled=True)  6.36 us
    all_to_all x1, starting transfers between devices, shards(): mods = lax.all_to_all(parts, 'dp', 0, 0, tiled=True)  3.55 us
    pallas_call x1, Pallas kernels, shards(): pl.pallas_call(part_kernel, out_shape=jax.ShapeDtypeStruct((count, 2, col...  2.94 us
    ppermute x2, waiting for transfers between devices, shards(): ada_other, fin_other = (swap(ada), swap(final_ada))  1.46 us
  transfers between devices with their start and end apart: 7, of which 3 were waited for; matrix products, arithmetic and copies ran while one was open for 19% of the time, Pallas kernels for 6%

profile of v1, /device:TPU:0, one launch (start us, length us, event | category | flops | bytes accessed | tf_op | source)
XLA Modules:
  0.0 69.5 jit_solution(64095470337245136)
XLA Ops:
  0.6 0.6 collective-permute-start
  1.8 0.7 copy-done.12
  2.5 0.7 copy-done.13
  3.1 0.7 copy-done.15
  3.8 1.2 %shard_map.167 = f32[16,16,128]{2,1,0:T(8,128)} custom-call(s32[2]{0:T(128)S(1)} %pad_add_fusion.core_ref.place_ref, f32[2]{0:T(128)S(1)} %copy-done.13, f32[2]{0:T(128)S(1)} %copy-done.15, bf16[2,1152]{1,0:T(2,128)(2,1)S(1)} %copy-done.12), custom_call_target="tpu_custom_call" | custom-call | tf_op jit(solution)/shard_map/pallas_call | solution.py:255
  5.0 7.9 %all-to-all-start = ((f32[16,16,128]{2,1,0:T(8,128)}), f32[16,16,128]{2,1,0:T(8,128)S(1)}, u32[]{:S(2)}, u32[]{:S(2)}) async-start(f32[16,16,128]{2,1,0:T(8,128)} %shard_map.167), calls=%async_computation | async-start | bytes 262144 | tf_op jit(solution)/shard_map/all_to_all | solution.py:263
  13.2 1.5 %collective-permute-done.3.fin_other = bf16[72,1152]{1,0:T(8,128)(2,1)S(1)} collective-permute-done((bf16[72,1152]{1,0:T(8,128)(2,1)}, bf16[72,1152]{1,0:T(8,128)(2,1)S(1)}, u32[]{:S(2)}, u32[]{:S(2)}) %collective-permute-start.3) | collective-permute-done | bytes 165920 | tf_op jit(solution)/shard_map/ppermute | solution.py:251
  14.6 6.4 %all-to-all-done.heard_ref = f32[16,16,128]{2,1,0:T(8,128)S(1)} async-done(((f32[16,16,128]{2,1,0:T(8,128)}), f32[16,16,128]{2,1,0:T(8,128)S(1)}, u32[]{:S(2)}, u32[]{:S(2)}) %all-to-all-start) | async-done | bytes 131104 | tf_op jit(solution)/shard_map/all_to_all | solution.py:263
  21.0 1.7 %copy-done.2 = bf16[1152,1152]{1,0:T(8,128)(2,1)S(1)} copy-done((bf16[1152,1152]{1,0:T(8,128)(2,1)S(1)}, bf16[1152,1152]{1,0:T(8,128)(2,1)}, u32[]{:S(2)}) %copy-start.2) | copy-done | bytes 2654232
  22.7 1.1 %copy-done.5 = bf16[256,1152]{1,0:T(8,128)(2,1)S(1)} copy-done((bf16[256,1152]{1,0:T(8,128)(2,1)S(1)}, bf16[256,1152]{1,0:T(8,128)(2,1)}, u32[]{:S(2)}) %copy-start.5) | copy-done | bytes 589848
  23.8 0.9 %copy-done.6 = bf16[1,72,1728]{2,1,0:T(8,128)(2,1)S(1)} copy-done((bf16[1,72,1728]{2,1,0:T(8,128)(2,1)S(1)}, bf16[1,72,1728]{2,1,0:T(8,128)(2,1)}, u32[]{:S(2)}) %copy-start.6) | copy-done | bytes 248856
  24.7 0.9 %copy-done.7 = bf16[72,1152]{1,0:T(8,128)(2,1)S(1)} copy-done((bf16[72,1152]{1,0:T(8,128)(2,1)S(1)}, bf16[72,1152]{1,0:T(8,128)(2,1)}, u32[]{:S(2)}) %copy-start.7) | copy-done | bytes 165912
  25.7 0.7 copy-done.18
  26.3 2.9 %shard_map.168 = bf16[16,2,5888]{2,1,0:T(2,128)(2,1)} custom-call(s32[2]{0:T(128)S(1)} %pad_add_fusion.core_ref.place_ref, f32[16,16,128]{2,1,0:T(8,128)S(1)} %all-to-all-done.heard_ref, f32[1,128]{1,0:T(1,128)S(1)} %copy-done.18, bf16[256,1152]{1,0:T(8,128)(2,1)S(1)} %copy-done.5, bf16[1152,1152]{1,0:T(8,128)(2,1)S(1)} %copy-done.2, ...), custom_call_target="tpu_custom_call" | custom-call | tf_op jit(solution)/shard_map/pallas_call | solution.py:269
  29.3 3.5 %all-to-all-start.1 = ((bf16[16,2,5888]{2,1,0:T(2,128)(2,1)}), bf16[16,2,5888]{2,1,0:T(2,128)(2,1)S(1)}, u32[]{:S(2)}, u32[]{:S(2)}) async-start(bf16[16,2,5888]{2,1,0:T(2,128)(2,1)} %shard_map.168), calls=%async_computation.1 | async-start | bytes 753664 | tf_op jit(solution)/shard_map/all_to_all | solution.py:277
  32.8 6.6 %copy.20 = bf16[1,1152,3,576]{3,1,2,0:T(8,128)(2,1)} copy(bf16[1,1152,3,576]{1,3,2,0:T(8,128)(2,1)} %param.25) | data formatting | bytes 7962624 | tf_op args[9]
  39.5 6.7 %copy.22.qkv_other = bf16[3,1152,576]{2,1,0:T(8,128)(2,1)} copy(bf16[3,1152,576]{1,2,0:T(8,128)(2,1)} %collective-permute-done) | data formatting | bytes 7962624 | tf_op jit(solution)/shard_map/ppermute | solution.py:252
  46.3 2.2 %copy-done = bf16[1,1152,3,576]{3,1,2,0:T(8,128)(2,1)S(1)} copy-done((bf16[1,1152,3,576]{3,1,2,0:T(8,128)(2,1)S(1)}, bf16[1,1152,3,576]{3,1,2,0:T(8,128)(2,1)}, u32[]{:S(2)}) %copy-start) | copy-done | bytes 3981336
  48.5 2.3 %copy-done.1 = bf16[3,1152,576]{2,1,0:T(8,128)(2,1)S(1)} copy-done((bf16[3,1152,576]{2,1,0:T(8,128)(2,1)S(1)}, bf16[3,1152,576]{2,1,0:T(8,128)(2,1)}, u32[]{:S(2)}) %copy-start.1) | copy-done | bytes 3981336
  50.8 1.3 %copy-done.4 = f32[256,1152]{1,0:T(8,128)S(1)} copy-done((f32[256,1152]{1,0:T(8,128)S(1)}, f32[256,1152]{1,0:T(8,128)}, u32[]{:S(2)}) %copy-start.4) | copy-done | bytes 1179672
  52.0 14.9 %shard_map.169 = f32[40,128]{1,0:T(8,128)S(1)} custom-call(s32[2]{0:T(128)S(1)} %pad_add_fusion.core_ref.place_ref, f32[2]{0:T(128)S(1)} %copy-done.14, f32[2]{0:T(128)S(1)} %copy-done.16, s32[2]{0:T(128)S(1)} %copy-done.17, f32[2,4096]{1,0:T(2,128)S(1)} %copy-done.10, f32[2,4096]{1,0:T(2,128)S(1)} %copy-done.11, f32[256,1152]{1,0:T(8,128)S(1)} %copy-done.4, ...), custom_call_target="tpu_custom_call" | custom-call | tf_op jit(solution)/shard_map/pallas_call | solution.py:283
  67.0 1.2 %collective-permute-done.4 = f32[40,128]{1,0:T(8,128)S(1)} collective-permute-done((f32[40,128]{1,0:T(8,128)S(1)}, f32[40,128]{1,0:T(8,128)S(1)}, u32[]{:S(2)}, u32[]{:S(2)}) %collective-permute-start.4) | collective-permute-done | bytes 20512 | tf_op jit(solution)/shard_map/ppermute | solution.py:304
  68.2 0.6 fusion.2
  68.8 0.6 copy.26
  (38 shorter events, 0.9 us)
Async XLA Ops:
  0.6 38.8 %collective-permute-start = (bf16[3,1152,576]{1,2,0:T(8,128)(2,1)}, bf16[3,1152,576]{1,2,0:T(8,128)(2,1)}, u32[]{:S(2)}, u32[]{:S(2)}) collective-permute-start(bf16[3,1152,576]{1,2,0:T(8,128)(2,1)} %bitcast.26), channel_id=1, source_target_pairs={{0,1},{1,0},{2,3},{3,2},{4,5},{5,4},{6,7},{7,6},{8,9},{9,8},{10,11... | collective-permute-start | bytes 11943944 | tf_op jit(solution)/shard_map/ppermute | solution.py:252
  1.2 45.0 %collective-permute-start.1 = (bf16[576,1152]{1,0:T(8,128)(2,1)}, bf16[576,1152]{1,0:T(8,128)(2,1)S(1)}, u32[]{:S(2)}, u32[]{:S(2)}) collective-permute-start(bf16[576,1152]{1,0:T(8,128)(2,1)} %bitcast.21), channel_id=1, source_target_pairs={{0,1},{1,0},{2,3},{3,2},{4,5},{5,4},{6,7},{7,6},{8,9},{9,8},{10,11... | collective-permute-start | bytes 3981320 | tf_op jit(solution)/shard_map/ppermute | solution.py:252
  1.3 19.7 %collective-permute-start.2 = (bf16[72,1728]{1,0:T(8,128)(2,1)}, bf16[72,1728]{1,0:T(8,128)(2,1)S(1)}, u32[]{:S(2)}, u32[]{:S(2)}) collective-permute-start(bf16[72,1728]{1,0:T(8,128)(2,1)} %bitcast.23), channel_id=1, source_target_pairs={{0,1},{1,0},{2,3},{3,2},{4,5},{5,4},{6,7},{7,6},{8,9},{9,8},{10,11... | collective-permute-start | bytes 746504 | tf_op jit(solution)/shard_map/ppermute | solution.py:251
  1.8 0.7 copy-start.12
  2.5 0.7 copy-start.13
  5.0 16.0 %all-to-all-start = ((f32[16,16,128]{2,1,0:T(8,128)}), f32[16,16,128]{2,1,0:T(8,128)S(1)}, u32[]{:S(2)}, u32[]{:S(2)}) async-start(f32[16,16,128]{2,1,0:T(8,128)} %shard_map.167), calls=%async_computation | async-start | bytes 262144 | tf_op jit(solution)/shard_map/all_to_all | solution.py:263
  12.9 1.7 %collective-permute-start.3 = (bf16[72,1152]{1,0:T(8,128)(2,1)}, bf16[72,1152]{1,0:T(8,128)(2,1)S(1)}, u32[]{:S(2)}, u32[]{:S(2)}) collective-permute-start(bf16[72,1152]{1,0:T(8,128)(2,1)} %fin_own.1), channel_id=1, source_target_pairs={{0,1},{1,0},{2,3},{3,2},{4,5},{5,4},{6,7},{7,6},{8,9},{9,8},{10,11... | collective-permute-start | bytes 497672 | tf_op jit(solution)/shard_map/ppermute | solution.py:251
  21.0 1.8 %copy-start.2 = (bf16[1152,1152]{1,0:T(8,128)(2,1)S(1)}, bf16[1152,1152]{1,0:T(8,128)(2,1)}, u32[]{:S(2)}) copy-start(bf16[1152,1152]{1,0:T(8,128)(2,1)} %time_out_ref.1) | copy-start | bytes 7962628
  22.7 1.1 %copy-start.5 = (bf16[256,1152]{1,0:T(8,128)(2,1)S(1)}, bf16[256,1152]{1,0:T(8,128)(2,1)}, u32[]{:S(2)}) copy-start(bf16[256,1152]{1,0:T(8,128)(2,1)} %time_in_ref.1) | copy-start | bytes 1769476
  23.8 0.9 %copy-start.6 = (bf16[1,72,1728]{2,1,0:T(8,128)(2,1)S(1)}, bf16[1,72,1728]{2,1,0:T(8,128)(2,1)}, u32[]{:S(2)}) copy-start(bf16[1,72,1728]{2,1,0:T(8,128)(2,1)} %param.27) | copy-start | bytes 746500
  24.7 0.9 %copy-start.7 = (bf16[72,1152]{1,0:T(8,128)(2,1)S(1)}, bf16[72,1152]{1,0:T(8,128)(2,1)}, u32[]{:S(2)}) copy-start(bf16[72,1152]{1,0:T(8,128)(2,1)} %fin_own.1) | copy-start | bytes 497668
  29.3 16.9 %all-to-all-start.1 = ((bf16[16,2,5888]{2,1,0:T(2,128)(2,1)}), bf16[16,2,5888]{2,1,0:T(2,128)(2,1)S(1)}, u32[]{:S(2)}, u32[]{:S(2)}) async-start(bf16[16,2,5888]{2,1,0:T(2,128)(2,1)} %shard_map.168), calls=%async_computation.1 | async-start | bytes 753664 | tf_op jit(solution)/shard_map/all_to_all | solution.py:277
  39.4 6.8 %copy-start.3 = (bf16[1,1152,576]{1,2,0:T(8,128)(2,1)S(1)}, bf16[1,1152,576]{1,2,0:T(8,128)(2,1)}, u32[]{:S(2)}) copy-start(bf16[1,1152,576]{1,2,0:T(8,128)(2,1)} %param.26) | copy-start | bytes 3981316
  39.4 6.8 %copy-start.8 = (bf16[16,1152]{1,0:T(8,128)(2,1)S(1)}, bf16[16,1152]{1,0:T(8,128)(2,1)}, u32[]{:S(2)}) copy-start(bf16[16,1152]{1,0:T(8,128)(2,1)} %patch_ref.1) | copy-start | bytes 110596
  39.4 6.8 %copy-start.9 = (bf16[1152,16]{0,1:T(8,128)(2,1)S(1)}, bf16[1152,16]{0,1:T(8,128)(2,1)}, u32[]{:S(2)}) copy-start(bf16[1152,16]{0,1:T(8,128)(2,1)} %param.29) | copy-start | bytes 110596
  39.4 6.8 %copy-start.10 = (f32[2,4096]{1,0:T(2,128)S(1)}, f32[2,4096]{1,0:T(2,128)}, u32[]{:S(2)}) copy-start(f32[2,4096]{1,0:T(2,128)} %cur_ref.1) | copy-start | bytes 98308
  39.4 6.8 %copy-start.11 = (f32[2,4096]{1,0:T(2,128)S(1)}, f32[2,4096]{1,0:T(2,128)}, u32[]{:S(2)}) copy-start(f32[2,4096]{1,0:T(2,128)} %noise_ref.1) | copy-start | bytes 98308
  39.4 6.8 %copy-start.14 = (f32[2]{0:T(128)S(1)}, f32[2]{0:T(128)}, u32[]{:S(2)}) copy-start(f32[2]{0:T(128)} %time_ref.3) | copy-start | bytes 28
  39.4 6.8 %copy-start.16 = (f32[2]{0:T(128)S(1)}, f32[2]{0:T(128)}, u32[]{:S(2)}) copy-start(f32[2]{0:T(128)} %step_ref.3) | copy-start | bytes 28
  39.4 6.8 %copy-start.17 = (s32[2]{0:T(128)S(1)}, s32[2]{0:T(128)}, u32[]{:S(2)}) copy-start(s32[2]{0:T(128)} %accept_ref.1) | copy-start | bytes 28
  46.2 2.3 %copy-start = (bf16[1,1152,3,576]{3,1,2,0:T(8,128)(2,1)S(1)}, bf16[1,1152,3,576]{3,1,2,0:T(8,128)(2,1)}, u32[]{:S(2)}) copy-start(bf16[1,1152,3,576]{3,1,2,0:T(8,128)(2,1)} %copy.20) | copy-start | bytes 11943940
  48.5 2.3 %copy-start.1 = (bf16[3,1152,576]{2,1,0:T(8,128)(2,1)S(1)}, bf16[3,1152,576]{2,1,0:T(8,128)(2,1)}, u32[]{:S(2)}) copy-start(bf16[3,1152,576]{2,1,0:T(8,128)(2,1)} %copy.22.qkv_other) | copy-start | bytes 11943940
  50.8 1.3 %copy-start.4 = (f32[256,1152]{1,0:T(8,128)S(1)}, f32[256,1152]{1,0:T(8,128)}, u32[]{:S(2)}) copy-start(f32[256,1152]{1,0:T(8,128)} %constant.15.clone.pos_ref) | copy-start | bytes 3538948
  66.9 1.3 %collective-permute-start.4 = (f32[40,128]{1,0:T(8,128)S(1)}, f32[40,128]{1,0:T(8,128)S(1)}, u32[]{:S(2)}, u32[]{:S(2)}) collective-permute-start(f32[40,128]{1,0:T(8,128)S(1)} %shard_map.169), channel_id=1, source_target_pairs={{0,1},{1,0},{2,3},{3,2},{4,5},{5,4},{6,7},{7,6},{8,9},{9,8},{10,11... | collective-permute-start | bytes 61448 | tf_op jit(solution)/shard_map/ppermute | solution.py:304
  (2 other events, 1.3 us)

commit v2 on v1

v2 whole, which is shorter than its diff:
```python
import functools
import math

import jax
import jax.numpy as jnp
import numpy as np
from jax import lax
from jax.experimental import pallas as pl
from jax.experimental.pallas import tpu as pltpu
from jax.sharding import PartitionSpec as P

HEAD_DIM = 72
LANES = 128
ROWS = 8
SUB = 16
AHEAD = 2
SLOTS = 4
GRANT = 60 << 20

beta_low = 0.1
beta_high = 20.0
tol_abs = 0.0078
tol_rel = 0.05
norm_eps = 1e-06

f32 = jnp.float32
bf16 = jnp.bfloat16
VM = pl.BlockSpec(memory_space=pltpu.VMEM)
HBM = pl.BlockSpec(memory_space=pltpu.HBM)
SM = pl.BlockSpec(memory_space=pltpu.SMEM)


def up(size, unit):
    return -(-size // unit) * unit


def mm(a, b):
    return lax.dot_general(a, b, (((1,), (0,)), ((), ())), preferred_element_type=f32)


def mm_t(a, b):
    return lax.dot_general(a, b, (((1,), (1,)), ((), ())), preferred_element_type=f32)


def start_copies(sources, targets, sems):
    copies = [
        pltpu.make_async_copy(source, target, sems.at[i])
        for i, (source, target) in enumerate(zip(sources, targets))
    ]
    for copy in copies:
        copy.start()
    return copies


def like(arrays):
    return [pltpu.VMEM(a.shape, a.dtype) for a in arrays]


def silu(v):
    return v / (1.0 + jnp.exp(-v))


def position_table(token_count, width):
    half = width // 2
    rates = np.exp(-math.log(10000.0) * np.arange(half) / half)
    angles = np.arange(token_count)[:, None] * rates[None, :]
    return np.concatenate([np.sin(angles), np.cos(angles)], axis=1).astype(np.float32)


def tell_kernel(time_hbm, step_hbm, labels_hbm, out_ref, time_ref, step_ref, labels_ref, block, sems):
    copies = start_copies(
        (time_hbm, step_hbm, labels_hbm), (time_ref, step_ref, labels_ref), sems
    )
    block[...] = jnp.zeros_like(block)
    for copy in copies:
        copy.wait()
    mine = lax.axis_index("tensor")
    tiles = labels_ref.shape[1] // LANES
    both = labels_ref[...].astype(f32)
    row = jnp.where(mine == 0, both[0:1], both[1:2])
    for tile in range(tiles):
        block[tile : tile + 1, :] = row[:, tile * LANES : (tile + 1) * LANES]
    now = time_ref[mine]
    later = now - step_ref[mine]
    block[tiles : tiles + 1, :] = jnp.full((1, LANES), now, f32)
    block[tiles + 1 : tiles + 2, :] = jnp.full((1, LANES), later, f32)
    for dest in range(out_ref.shape[0]):
        out_ref[dest] = block[...]


def part_kernel(heard_ref, *refs):
    sources, out_ref, sems = refs[:10], refs[10], refs[-1]
    time_in_ref, time_out_ref, ada_near, ada_far, fin_near, fin_far, part = refs[11:18]
    own_rows = sources[2].shape[0]
    second = up(own_rows, SUB)
    stacks = (ada_near, ada_far, fin_near, fin_far)
    stages = refs[18:-1]
    copies = [
        pltpu.make_async_copy(sources[0], time_in_ref, sems.at[0]),
        pltpu.make_async_copy(sources[1], time_out_ref, sems.at[1]),
    ]
    for at, source in enumerate(sources[2:]):
        stack = stacks[at // 2]
        first = at % 2 * second
        target = stages[at] if stages else stack.at[pl.ds(first, own_rows), :]
        copies.append(pltpu.make_async_copy(source, target, sems.at[2 + at]))
    for copy in copies:
        copy.start()
    count = heard_ref.shape[0]
    width = time_out_ref.shape[0]
    tiles = width // LANES
    labels = jnp.concatenate([heard_ref[:, tile, :] for tile in range(tiles)], axis=1)
    labels = jnp.concatenate([labels, labels], axis=0)
    moments = jnp.concatenate([heard_ref[:, tiles, :], heard_ref[:, tiles + 1, :]], axis=0)
    half_freq = time_in_ref.shape[0] // 2
    index = lax.broadcasted_iota(jnp.int32, (1, half_freq), 1).astype(f32)
    rates = jnp.exp(index * (-math.log(10000.0) / half_freq))
    angles = 1000.0 * moments * rates
    features = jnp.concatenate([jnp.cos(angles), jnp.sin(angles)], axis=1).astype(bf16)
    place = lax.axis_index("dp")
    pair = place + 1 - 2 * lax.rem(place, 2)
    depth = ada_near.shape[0]
    pick_shape = (width, depth)
    at_row = lax.broadcasted_iota(jnp.int32, pick_shape, 0)
    at_lane = lax.broadcasted_iota(jnp.int32, pick_shape, 1)
    mine = (at_lane < own_rows) & (at_row == at_lane + place * own_rows)
    theirs = (at_lane >= second) & (at_lane < second + own_rows)
    theirs = theirs & (at_row == at_lane - second + pair * own_rows)
    pick = jnp.where(mine | theirs, 1.0, 0.0).astype(bf16)
    copies[0].wait()
    hidden = silu(mm(features, time_in_ref[...])).astype(bf16)
    copies[1].wait()
    cond = silu(labels + mm(hidden, time_out_ref[...])).astype(bf16)
    own_cond = mm(cond, pick).astype(bf16)
    low = lax.axis_index("tensor") == 0
    for copy in copies[2:]:
        copy.wait()
    for at, stage in enumerate(stages):
        first = at % 2 * second
        stacks[at // 2][first : first + own_rows, :] = stage[...]
    if second != own_rows:
        for stack in stacks:
            for first in (own_rows, second + own_rows):
                stack[first : first + second - own_rows, :] = jnp.zeros(
                    (second - own_rows, stack.shape[1]), bf16
                )
    wide = up(ada_near.shape[1], LANES)
    for at, near, far in ((0, ada_near, ada_far), (2 * wide, fin_near, fin_far)):
        a = mm(own_cond, near[...])
        b = mm(own_cond, far[...])
        used = a.shape[1]
        gap = up(used, LANES)
        part[:, at : at + used] = jnp.where(low, a, b)
        part[:, at + gap : at + gap + used] = jnp.where(low, b, a)
        if gap != used:
            part[:, at + used : at + gap] = jnp.zeros((2 * count, gap - used), f32)
            part[:, at + gap + used : at + 2 * gap] = jnp.zeros((2 * count, gap - used), f32)
    for dest in range(count):
        now_row = part[dest : dest + 1, :]
        later_row = part[count + dest : count + dest + 1, :]
        out_ref[dest] = jnp.concatenate([now_row, later_row], axis=0).astype(bf16)


def norm(v):
    width = v.shape[1]
    average = jnp.sum(v, axis=1, keepdims=True) * (1.0 / width)
    centred = v - average
    spread_sq = jnp.sum(centred * centred, axis=1, keepdims=True) * (1.0 / width)
    return centred * lax.rsqrt(spread_sq + norm_eps)


def step_kernel(
    time_hbm, step_hbm, accept_hbm, mods_ref, *refs,
):
    sources, out_ref, rest_refs = refs[:9], refs[9], refs[18:]
    cur_ref, noise_ref, patch_ref, pos_ref, qkv_own, qkv_other, out_all, proj_ref = refs[10:18]
    half = qkv_own.shape[1]
    targets = (
        cur_ref, noise_ref, patch_ref, pos_ref, qkv_own, qkv_other,
        out_all.at[pl.ds(0, half), :], out_all.at[pl.ds(half, half), :], proj_ref,
    )
    time_ref, step_ref, accept_ref, sems, *work = rest_refs
    early = start_copies(
        (time_hbm, step_hbm, accept_hbm), (time_ref, step_ref, accept_ref), sems.at[pl.ds(9, 3)]
    )
    copies = [pltpu.make_async_copy(s, t, sems.at[i]) for i, (s, t) in enumerate(zip(sources, targets))]
    for at in (0, 1, 2, 8, 3, 4, 5, 6, 7):
        copies[at].start()
    for copy in early + copies[:3] + copies[8:]:
        copy.wait()
    step_body(
        time_ref, step_ref, accept_ref, cur_ref, noise_ref, pos_ref, patch_ref,
        qkv_own, qkv_other, out_all, proj_ref, mods_ref, out_ref, copies[3:8], *work,
    )


def step_body(
    time_ref, step_ref, accept_ref, cur_ref, noise_ref, pos_ref, patch_ref,
    qkv_own, qkv_other, out_all, proj_ref, mods_ref, out_ref, copies,
    cur32, nse32, state32, guess32, modv, patch8, proj8, stream, inner, query, keys, value, mixed,
    scores, probs, turned,
):
    mine = lax.axis_index("tensor")
    low_core = mine == 0
    lat_rows = cur32.shape[0]
    tokens, width = stream.shape
    half = qkv_own.shape[1]
    heads = half // HEAD_DIM
    count = mods_ref.shape[0]
    vals = patch_ref.shape[0]
    reps = LANES // vals

    for row in range(lat_rows):
        lanes = slice(row * LANES, (row + 1) * LANES)
        cur32[row : row + 1, :] = jnp.where(low_core, cur_ref[0:1, lanes], cur_ref[1:2, lanes])
        nse32[row : row + 1, :] = jnp.where(low_core, noise_ref[0:1, lanes], noise_ref[1:2, lanes])
    for rep in range(reps):
        patch8[rep * vals : (rep + 1) * vals, :] = patch_ref[...]
        proj8[rep * vals : (rep + 1) * vals, :] = proj_ref[...]
    query[:, half:, :] = jnp.zeros((2, query.shape[1] - half, tokens), bf16)
    keys[:, :, half:] = jnp.zeros((2, tokens, keys.shape[2] - half), bf16)

    total = mods_ref[0].astype(f32)
    for source in range(1, count):
        total = total + mods_ref[source].astype(f32)
    lay_cols = 3 * width // 2
    wide = up(lay_cols, LANES)
    low = total[:, :wide]
    high = total[:, wide : 2 * wide]
    lane = lax.broadcasted_iota(jnp.int32, (2, width), 1)
    rest = low[:, width:]
    rest = jnp.concatenate([rest, jnp.zeros((2, width - rest.shape[1]), f32)], axis=1)
    split = lay_cols - width
    scale_attn = jnp.where(lane < split, rest, pltpu.roll(high[:, :width], split, 1))
    gate_attn = pltpu.roll(high, wide - (width - split), 1)[:, :width]
    for moment in range(2):
        row = slice(moment, moment + 1)
        modv[moment, 0:1, :] = low[row, :width]
        modv[moment, 1:2, :] = 1.0 + scale_attn[row]
        modv[moment, 2:3, :] = gate_attn[row]
        modv[moment, 3:4, :] = total[row, 2 * wide : 2 * wide + width]
        modv[moment, 4:5, :] = 1.0 + total[row, 2 * wide + width : 2 * wide + 2 * width]

    now = jnp.full((1, LANES), time_ref[mine], f32)
    step = jnp.full((1, LANES), step_ref[mine], f32)
    later = now - step

    def beta_at(m):
        return beta_low + (beta_high - beta_low) * m

    def drift(values, m, guess):
        rate = beta_at(m)
        integral = beta_low * m + 0.5 * (beta_high - beta_low) * m * m
        return 0.5 * rate * values - rate * guess / jnp.sqrt(1.0 - jnp.exp(-integral))

    spread = jnp.sqrt(step * beta_at(now)) * nse32[...]
    group = lax.broadcasted_iota(jnp.int32, (tokens, LANES), 1) // vals
    own_slot = group == lax.broadcasted_iota(jnp.int32, (tokens, LANES), 0) % reps
    exp_scale = HEAD_DIM**-0.5 * math.log2(math.e)

    def fetched(index, which):
        @pl.when(index == 0)
        def _():
            copies[which].wait()

    ones = jnp.ones((ROWS, tokens), f32)

    def project(part, kind, weight):
        raw = mm_t(weight[kind], inner[...])
        if kind == 0:
            query[part, :half, :] = raw.astype(bf16)
        elif kind == 1:
            keys[part, :, :half] = raw.astype(bf16).T
        else:
            for head in range(heads):
                rows = slice(head * HEAD_DIM, (head + 1) * HEAD_DIM)
                value[part, head] = jnp.concatenate([raw[rows], ones], axis=0).astype(bf16)

    def score(at):
        part, head = divmod(at, heads)
        begin = head * HEAD_DIM
        lo = begin // LANES * LANES
        hi = up(begin + HEAD_DIM, LANES)
        row = lax.broadcasted_iota(jnp.int32, (hi - lo, tokens), 0) + lo
        inside = (row >= begin) & (row < begin + HEAD_DIM)
        q = jnp.where(inside, query[part, lo:hi, :], jnp.zeros((), bf16))
        scores[at % SLOTS] = mm(keys[part, :, lo:hi], q)

    def evaluate(index, carry):
        del carry
        x = state32[...]
        tok = jnp.broadcast_to(x[:, None, :], (lat_rows, reps, LANES)).reshape(tokens, LANES)
        tok = jnp.where(own_slot, tok, 0.0).astype(bf16)
        fetched(index, 0)
        stream[...] = mm(tok, patch8[...]) + pos_ref[...]
        inner[...] = (norm(stream[...]) * modv[index, 1:2, :] + modv[index, 0:1, :]).astype(bf16)
        fetched(index, 1)
        for kind in range(3):
            project(0, kind, qkv_own)
        fetched(index, 2)
        for at in range(AHEAD):
            score(at)
        got = {}
        for at in range(2 * heads):
            if at < 3:
                project(1, (1, 0, 2)[at], qkv_other)
            raw = scores[at % SLOTS]
            top = jnp.max(raw, axis=0, keepdims=True)
            probs[at % 2] = jnp.exp2((raw - top) * exp_scale).astype(bf16)
            if at + AHEAD < 2 * heads:
                score(at + AHEAD)
            part, head = divmod(at, heads)
            mix = mm(value[part, head], probs[at % 2])
            got[at] = mix[:HEAD_DIM] * (1.0 / mix[HEAD_DIM : HEAD_DIM + 1])
            if at % 2:
                pair = jnp.concatenate([got.pop(at - 1), got.pop(at)], axis=0)
                first = (at - 1) * HEAD_DIM
                mixed[first : first + 2 * HEAD_DIM, :] = pair.astype(bf16)
        fetched(index, 3)
        fetched(index, 4)
        turned[...] = mixed[...].T
        stream[...] += modv[index, 2:3, :] * mm(turned[...], out_all[...])
        inner[...] = (norm(stream[...]) * modv[index, 4:5, :] + modv[index, 3:4, :]).astype(bf16)
        guess = jnp.where(own_slot, mm_t(inner[...], proj8[...]), 0.0)
        guess = jnp.sum(guess.reshape(lat_rows, reps, LANES), axis=1)
        guess32[index] = guess

        @pl.when(index == 0)
        def _():
            state32[...] = cur32[...] + step * drift(cur32[...], now, guess) + spread

        return 0

    state32[...] = cur32[...]
    lax.fori_loop(0, 2, evaluate, 0)

    cur = cur32[...]
    euler = state32[...]
    drift_now = drift(cur, now, guess32[0])
    drift_later = drift(euler, later, guess32[1])
    heun = cur + 0.5 * step * (drift_now + drift_later) + spread
    scale_ref = jnp.maximum(tol_abs, tol_rel * jnp.maximum(jnp.abs(heun), jnp.abs(cur)))
    gap = (euler - heun) / scale_ref
    square = jnp.sum(jnp.sum(gap * gap, axis=1, keepdims=True), axis=0, keepdims=True)
    error = jnp.sqrt(square / (lat_rows * LANES))
    out_ref[:lat_rows, :] = jnp.where(accept_ref[mine] == 1, heun, cur)
    out_ref[lat_rows:, :] = jnp.broadcast_to(error, (ROWS, LANES))


def join_kernel(done_ref, other_ref, state_ref, error_ref):
    low = lax.axis_index("tensor") == 0
    lat_rows = state_ref.shape[1] // LANES
    done, other = done_ref[...], other_ref[...]
    first, second = jnp.where(low, done, other), jnp.where(low, other, done)
    for row in range(lat_rows):
        lanes = slice(row * LANES, (row + 1) * LANES)
        state_ref[0:1, lanes] = first[row : row + 1]
        state_ref[1:2, lanes] = second[row : row + 1]
    error_ref[0] = jnp.max(first[lat_rows:])
    error_ref[1] = jnp.max(second[lat_rows:])


def shards(
    current, noise_draw, labels, time_now, step_size, accept, patch_weight, time_in,
    time_out, qkv_weight, out_weight, ada_weight, final_ada, final_proj,
):
    members = lax.axis_size("dp")
    count = members // 2
    groups = [[2 * i + side for i in range(count)] for side in range(2)]
    trade = functools.partial(
        lax.ppermute, axis_name="dp", perm=[(i, i ^ 1) for i in range(members)]
    )
    width = time_out.shape[0]
    latent = current.shape[1]
    vals = patch_weight.shape[0]
    tokens = latent // vals
    half = qkv_weight.shape[3]
    swap = functools.partial(lax.ppermute, axis_name="tensor", perm=[(0, 1), (1, 0)])

    qkv = qkv_weight[0].transpose(1, 2, 0)
    out = out_weight[0].T
    ada = ada_weight[0]

    ada_pair, fin_pair = trade(ada), trade(final_ada)
    ada_other, fin_other = swap(ada), swap(final_ada)
    qkv_other, out_other = swap(qkv), swap(out)

    tell_rows = up(width // LANES + 2, ROWS)
    told = pl.pallas_call(
        tell_kernel,
        out_shape=jax.ShapeDtypeStruct((count, tell_rows, LANES), f32),
        in_specs=[HBM, HBM, HBM],
        out_specs=VM,
        scratch_shapes=[
            pltpu.SMEM(time_now.shape, f32),
            pltpu.SMEM(step_size.shape, f32),
            pltpu.VMEM(labels.shape, labels.dtype),
            pltpu.VMEM((tell_rows, LANES), f32),
            pltpu.SemaphoreType.DMA((3,)),
        ],
        compiler_params=pltpu.CompilerParams(vmem_limit_bytes=GRANT),
    )(time_now, step_size, labels)
    heard = lax.all_to_all(told, "dp", 0, 0, axis_index_groups=groups, tiled=True)
    heard, ada_pair, fin_pair = lax.optimization_barrier((heard, ada_pair, fin_pair))
    ada_pair_other, fin_pair_other = swap(ada_pair), swap(fin_pair)

    cols = 2 * up(ada.shape[1], LANES) + 2 * final_ada.shape[1]
    depth = 2 * up(ada.shape[0], SUB)
    near = (
        time_in, time_out, ada, ada_pair, ada_other, ada_pair_other,
        final_ada, fin_pair, fin_other, fin_pair_other,
    )
    parts = pl.pallas_call(
        part_kernel,
        out_shape=jax.ShapeDtypeStruct((count, 2, cols), bf16),
        in_specs=[VM] + [HBM] * len(near),
        out_specs=VM,
        scratch_shapes=like(near[:2])
        + [pltpu.VMEM((depth, a.shape[1]), bf16) for a in (ada, ada, final_ada, final_ada)]
        + [pltpu.VMEM((2 * count, cols), f32)]
        + (like(near[2:]) if ada.shape[0] % ROWS else [])
        + [pltpu.SemaphoreType.DMA((len(near),))],
        compiler_params=pltpu.CompilerParams(vmem_limit_bytes=GRANT),
    )(heard, *near)
    mods = lax.all_to_all(parts, "dp", 0, 0, axis_index_groups=groups, tiled=True)

    lat_rows = latent // LANES
    padded = up(half, LANES)
    positions = jnp.asarray(position_table(tokens, width))
    small = pltpu.VMEM((lat_rows, LANES), f32)
    held = (
        current, noise_draw, patch_weight, positions, qkv, qkv_other, out, out_other, final_proj.T
    )
    done = pl.pallas_call(
        step_kernel,
        out_shape=jax.ShapeDtypeStruct((lat_rows + ROWS, LANES), f32),
        in_specs=[HBM, HBM, HBM, VM] + [HBM] * len(held),
        out_specs=VM,
        scratch_shapes=like(held[:6])
        + [pltpu.VMEM((width, width), bf16)]
        + like(held[8:])
        + [
            pltpu.SMEM(time_now.shape, f32),
            pltpu.SMEM(step_size.shape, f32),
            pltpu.SMEM(accept.shape, accept.dtype),
            pltpu.SemaphoreType.DMA((len(held) + 3,)),
            small, small, small,
            pltpu.VMEM((2, lat_rows, LANES), f32),
            pltpu.VMEM((2, ROWS, width), f32),
            pltpu.VMEM((LANES, width), bf16),
            pltpu.VMEM((LANES, width), bf16),
            pltpu.VMEM((tokens, width), f32),
            pltpu.VMEM((tokens, width), bf16),
            pltpu.VMEM((2, padded, tokens), bf16),
            pltpu.VMEM((2, tokens, padded), bf16),
            pltpu.VMEM((2, half // HEAD_DIM, HEAD_DIM + ROWS, tokens), bf16),
            pltpu.VMEM((2 * half, tokens), bf16),
            pltpu.VMEM((SLOTS, tokens, tokens), f32),
            pltpu.VMEM((2, tokens, tokens), bf16),
            pltpu.VMEM((tokens, 2 * half), bf16),
        ],
        compiler_params=pltpu.CompilerParams(vmem_limit_bytes=GRANT),
    )(
        time_now, step_size, accept, mods, *held,
    )
    other = swap(done)
    return pl.pallas_call(
        join_kernel,
        out_shape=(
            jax.ShapeDtypeStruct((2, latent), f32),
            jax.ShapeDtypeStruct((2,), f32),
        ),
        in_specs=[VM, VM],
        out_specs=(VM, SM),
    )(done, other)


def solution(mesh):
    in_specs = (
        P("dp", None),
        P("dp", None),
        P("dp", None),
        P("dp"),
        P("dp"),
        P("dp"),
        P(),
        P(),
        P(),
        P(None, None, None, "tensor"),
        P(None, None, "tensor"),
        P(None, "dp", "tensor"),
        P("dp", "tensor"),
        P(),
    )
    out_specs = (P("dp", None), P("dp"))
    return jax.shard_map(shards, mesh=mesh, in_specs=in_specs, out_specs=out_specs, check_vma=False)
```

time: 70.3 us -> 62 us (0.88)
  local copies, waits for them, and re-layouts: 27.1 us -> 3.03 us
  blocking collectives: 0 us -> 12.4 us
  Pallas kernels: 19.1 us -> 25.3 us
  starting transfers between devices: 12.8 us -> 10.5 us
    unnamed x40 -> x18, local copies, waits for them, and re-layouts: 20.4 us -> 3.03 us
    all_to_all x0 -> x1, blocking collectives: none -> 12.4 us  [shards(): lax.all_to_all(parts, 'dp', 0, 0, axis_index_groups=groups, tiled=True)]
    ppermute x1 -> x0, local copies, waits for them, and re-layouts: 6.7 us -> none  [shards(): qkv_other, out_other = (swap(qkv), swap(out))]
    all_to_all x2 -> x1, starting transfers between devices: 11.5 us -> 6.36 us  [shards(): lax.all_to_all(told, 'dp', 0, 0, axis_index_groups=groups, tiled=True)]
    ppermute x0 -> x4, waiting for transfers between devices: none -> 3.72 us  [the longest x2 2.47 us: shards(): ada_pair, fin_pair = (trade(ada), trade(final_ada))]
    ppermute x0 -> x4, starting transfers between devices: none -> 3.48 us  [the longest x2 2.93 us: shards(): ada_pair, fin_pair = (trade(ada), trade(final_ada))]
    pallas_call x1, Pallas kernels: 14.9 us -> 17.7 us  [shards(): pl.pallas_call(step_kernel, out_shape=jax.ShapeDtypeStruct((lat_rows + RO...]
    all_to_all x2 -> x1, waiting for transfers between devices: 6.36 us -> 4.42 us  [shards(): lax.all_to_all(told, 'dp', 0, 0, axis_index_groups=groups, tiled=True)]
  transfers between devices with their start and end apart: 7 -> 10, of which waited for: 3 -> 4; matrix products, arithmetic and copies ran while one was open for 19% -> 0% of each run, Pallas kernels for 6% -> 10%
where the time goes in v2:
time: 62 us; the launch traced here: 61.6 us
  Pallas kernels  25.3 us (41%)
  blocking collectives  12.4 us (20%)
  starting transfers between devices  10.5 us (17%)
  waiting for transfers between devices  9.54 us (15%)
  local copies, waits for them, and re-layouts  3.03 us (5%)
  between operations  0.75 us (1%)
    pallas_call x1, Pallas kernels, shards(): pl.pallas_call(step_kernel, out_shape=jax.ShapeDtypeStruct((lat_rows + RO...  17.7 us
    all_to_all x1, blocking collectives, shards(): lax.all_to_all(parts, 'dp', 0, 0, axis_index_groups=groups, tiled=True)  12.4 us
    all_to_all x1, starting transfers between devices, shards(): lax.all_to_all(told, 'dp', 0, 0, axis_index_groups=groups, tiled=True)  6.36 us
    pallas_call x1, Pallas kernels, shards(): pl.pallas_call(part_kernel, out_shape=jax.ShapeDtypeStruct((count, 2, col...  4.81 us
    all_to_all x1, waiting for transfers between devices, shards(): lax.all_to_all(told, 'dp', 0, 0, axis_index_groups=groups, tiled=True)  4.42 us
    unnamed x18, local copies, waits for them, and re-layouts  3.03 us
    ppermute x2, starting transfers between devices, shards(): ada_pair, fin_pair = (trade(ada), trade(final_ada))  2.93 us
    ppermute x2, waiting for transfers between devices, shards(): ada_pair, fin_pair = (trade(ada), trade(final_ada))  2.47 us
  transfers between devices with their start and end apart: 10, of which 4 were waited for; matrix products, arithmetic and copies ran while one was open for 0% of the time, Pallas kernels for 10%

profile of v2, /device:TPU:0, one launch (start us, length us, event | category | flops | bytes accessed | tf_op | source)
XLA Modules:
  0.0 61.6 jit_solution(3822531585308933228)
XLA Ops:
  0.6 0.6 collective-permute-start.6
  1.2 0.1 collective-permute-start.7
  1.3 2.9 %collective-permute-start = (bf16[72,1728]{1,0:T(8,128)(2,1)}, bf16[72,1728]{1,0:T(8,128)(2,1)S(1)}, u32[]{:S(2)}, u32[]{:S(2)}) collective-permute-start(bf16[72,1728]{1,0:T(8,128)(2,1)} %bitcast.12), channel_id=1, source_target_pairs={{0,2},{2,0},{4,6},{6,4},{8,10},{10,8},{12,14},{14,12},{16,18},{18,... | collective-permute-start | bytes 746504 | tf_op jit(solution)/shard_map/ppermute | solution.py:384
  4.2 0.0 collective-permute-start.1
  4.2 1.4 %shard_map.158 = f32[8,16,128]{2,1,0:T(8,128)} custom-call(f32[2]{0:T(128)} %time_hbm.3, f32[2]{0:T(128)} %step_hbm.3, bf16[2,1152]{1,0:T(2,128)(2,1)} %labels_hbm.1), custom_call_target="tpu_custom_call" | custom-call | tf_op jit(solution)/shard_map/pallas_call | solution.py:389
  5.6 6.4 %all-to-all-start = ((f32[8,16,128]{2,1,0:T(8,128)}), f32[8,16,128]{2,1,0:T(8,128)S(1)}, u32[]{:S(2)}, u32[]{:S(2)}) async-start(f32[8,16,128]{2,1,0:T(8,128)} %shard_map.158), calls=%async_computation | async-start | bytes 131072 | tf_op jit(solution)/shard_map/all_to_all | solution.py:403
  11.9 0.0 collective-permute-start.4
  11.9 2.5 %collective-permute-done.1.refs_7_ = bf16[72,1152]{1,0:T(8,128)(2,1)S(1)} collective-permute-done((bf16[72,1152]{1,0:T(8,128)(2,1)}, bf16[72,1152]{1,0:T(8,128)(2,1)S(1)}, u32[]{:S(2)}, u32[]{:S(2)}) %collective-permute-start.1) | collective-permute-done | bytes 165920 | tf_op jit(solution)/shard_map/ppermute | solution.py:384
  14.4 4.4 %all-to-all-done.heard_ref = f32[8,16,128]{2,1,0:T(8,128)S(1)} async-done(((f32[8,16,128]{2,1,0:T(8,128)}), f32[8,16,128]{2,1,0:T(8,128)S(1)}, u32[]{:S(2)}, u32[]{:S(2)}) %all-to-all-start) | async-done | bytes 65568 | tf_op jit(solution)/shard_map/all_to_all | solution.py:403
  18.8 0.0 collective-permute-done.refs_3_
  18.8 0.1 collective-permute-start.3
  18.9 0.0 collective-permute-done.4.refs_8_
  18.9 0.5 collective-permute-start.5
  19.4 1.2 %collective-permute-done.5.refs_9_ = bf16[72,1152]{1,0:T(8,128)(2,1)S(1)} collective-permute-done((bf16[72,1152]{1,0:T(8,128)(2,1)S(1)}, bf16[72,1152]{1,0:T(8,128)(2,1)S(1)}, u32[]{:S(2)}, u32[]{:S(2)}) %collective-permute-start.5) | collective-permute-done | bytes 165920 | tf_op jit(solution)/shard_map/ppermute | solution.py:405
  20.7 0.6 %copy-done.7 = bf16[72,1152]{1,0:T(8,128)(2,1)} copy-done((bf16[72,1152]{1,0:T(8,128)(2,1)}, bf16[72,1152]{1,0:T(8,128)(2,1)S(1)}, u32[]{:S(2)}) %copy-start.7) | copy-done | bytes 165912
  21.3 0.7 %copy-done.4 = bf16[72,1728]{1,0:T(8,128)(2,1)} copy-done((bf16[72,1728]{1,0:T(8,128)(2,1)}, bf16[72,1728]{1,0:T(8,128)(2,1)S(1)}, u32[]{:S(2)}) %copy-start.4) | copy-done | bytes 248856
  22.0 4.8 %shard_map.159 = bf16[8,2,5888]{2,1,0:T(2,128)(2,1)} custom-call(f32[8,16,128]{2,1,0:T(8,128)} %copy-done.1, bf16[256,1152]{1,0:T(8,128)(2,1)} %refs_0_.2, bf16[1152,1152]{1,0:T(8,128)(2,1)} %refs_1_.2, bf16[72,1728]{1,0:T(8,128)(2,1)} %bitcast.14, bf16[72,1728]{1,0:T(8,128)(2,1)} %copy-done.2, bf16[72,1728]{1,0:T(8,128)(2,1)} %copy-done.3, ...), custom_call_target="tpu_custom_call" | custom-call | tf_op jit(solution)/shard_map/pallas_call | solution.py:413
  26.9 12.4 %all_to_all.10.mods_ref = bf16[8,2,5888]{2,1,0:T(2,128)(2,1)} all-to-all(bf16[8,2,5888]{2,1,0:T(2,128)(2,1)} %shard_map.159), channel_id=1, replica_groups={{0,4,8,12,16,20,24,28},{2,6,10,14,18,22,26,30},{1,5,9,13,17,21,25,29},{..., dimensions={0} | all-to-all | bytes 376832 | tf_op jit(solution)/shard_map/all_to_all | solution.py:425
  39.3 1.1 %copy-done = bf16[576,1152]{1,0:T(8,128)(2,1)} copy-done((bf16[576,1152]{1,0:T(8,128)(2,1)}, bf16[576,1152]{1,0:T(8,128)(2,1)S(1)}, u32[]{:S(2)}) %copy-start) | copy-done | bytes 1327128
  40.4 17.7 %shard_map.160.done_ref = f32[40,128]{1,0:T(8,128)} custom-call(f32[2]{0:T(128)} %time_hbm.3, f32[2]{0:T(128)} %step_hbm.3, s32[2]{0:T(128)} %accept_hbm.1, bf16[8,2,5888]{2,1,0:T(2,128)(2,1)} %all_to_all.10.mods_ref, f32[2,4096]{1,0:T(2,128)} %refs_0_.3, f32[2,4096]{1,0:T(2,128)} %refs_1_.3, bf16[16,1152]{1,0:T(8,128)(2,1)} %refs_2_.1, ...), custom_call_target="tpu_custom_call" | custom-call | tf_op jit(solution)/shard_map/pallas_call | solution.py:434
  58.1 0.1 collective-permute-start.8
  58.2 1.4 %collective-permute-done.8.other_ref = f32[40,128]{1,0:T(8,128)S(1)} collective-permute-done((f32[40,128]{1,0:T(8,128)}, f32[40,128]{1,0:T(8,128)S(1)}, u32[]{:S(2)}, u32[]{:S(2)}) %collective-permute-start.8) | collective-permute-done | bytes 20512 | tf_op jit(solution)/shard_map/ppermute | solution.py:466
  59.6 0.6 copy-done.8
  60.2 1.4 %shard_map.161 = (f32[2,4096]{1,0:T(2,128)}, f32[2]{0:T(128)}) custom-call(f32[40,128]{1,0:T(8,128)} %shard_map.160.done_ref, f32[40,128]{1,0:T(8,128)} %copy-done.8), custom_call_target="tpu_custom_call" | custom-call | tf_op jit(solution)/shard_map/pallas_call | solution.py:467
  (19 shorter events, 0.0 us)
Async XLA Ops:
  0.6 38.7 %collective-permute-start.6 = (bf16[3,576,1152]{2,1,0:T(8,128)(2,1)}, bf16[3,576,1152]{2,1,0:T(8,128)(2,1)}, u32[]{:S(2)}, u32[]{:S(2)}) collective-permute-start(bf16[3,576,1152]{2,1,0:T(8,128)(2,1)} %bitcast.8), channel_id=1, source_target_pairs={{0,1},{1,0},{2,3},{3,2},{4,5},{5,4},{6,7},{7,6},{8,9},{9,8},{10,11... | collective-permute-start | bytes 11943944 | tf_op jit(solution)/shard_map/ppermute | solution.py:386
  1.2 38.1 %collective-permute-start.7 = (bf16[576,1152]{1,0:T(8,128)(2,1)}, bf16[576,1152]{1,0:T(8,128)(2,1)S(1)}, u32[]{:S(2)}, u32[]{:S(2)}) collective-permute-start(bf16[576,1152]{1,0:T(8,128)(2,1)} %bitcast.10), channel_id=1, source_target_pairs={{0,1},{1,0},{2,3},{3,2},{4,5},{5,4},{6,7},{7,6},{8,9},{9,8},{10,11... | collective-permute-start | bytes 3981320 | tf_op jit(solution)/shard_map/ppermute | solution.py:386
  1.3 17.6 %collective-permute-start = (bf16[72,1728]{1,0:T(8,128)(2,1)}, bf16[72,1728]{1,0:T(8,128)(2,1)S(1)}, u32[]{:S(2)}, u32[]{:S(2)}) collective-permute-start(bf16[72,1728]{1,0:T(8,128)(2,1)} %bitcast.12), channel_id=1, source_target_pairs={{0,2},{2,0},{4,6},{6,4},{8,10},{10,8},{12,14},{14,12},{16,18},{18,... | collective-permute-start | bytes 746504 | tf_op jit(solution)/shard_map/ppermute | solution.py:384
  4.2 10.2 %collective-permute-start.1 = (bf16[72,1152]{1,0:T(8,128)(2,1)}, bf16[72,1152]{1,0:T(8,128)(2,1)S(1)}, u32[]{:S(2)}, u32[]{:S(2)}) collective-permute-start(bf16[72,1152]{1,0:T(8,128)(2,1)} %refs_6_.1), channel_id=1, source_target_pairs={{0,2},{2,0},{4,6},{6,4},{8,10},{10,8},{12,14},{14,12},{16,18},{18,... | collective-permute-start | bytes 497672 | tf_op jit(solution)/shard_map/ppermute | solution.py:384
  5.6 13.3 %all-to-all-start = ((f32[8,16,128]{2,1,0:T(8,128)}), f32[8,16,128]{2,1,0:T(8,128)S(1)}, u32[]{:S(2)}, u32[]{:S(2)}) async-start(f32[8,16,128]{2,1,0:T(8,128)} %shard_map.158), calls=%async_computation | async-start | bytes 131072 | tf_op jit(solution)/shard_map/all_to_all | solution.py:403
  11.9 7.0 %collective-permute-start.4 = (bf16[72,1152]{1,0:T(8,128)(2,1)}, bf16[72,1152]{1,0:T(8,128)(2,1)S(1)}, u32[]{:S(2)}, u32[]{:S(2)}) collective-permute-start(bf16[72,1152]{1,0:T(8,128)(2,1)} %refs_6_.1), channel_id=1, source_target_pairs={{0,1},{1,0},{2,3},{3,2},{4,5},{5,4},{6,7},{7,6},{8,9},{9,8},{10,11... | collective-permute-start | bytes 497672 | tf_op jit(solution)/shard_map/ppermute | solution.py:385
  14.4 6.3 %copy-start.5 = (bf16[72,1152]{1,0:T(8,128)(2,1)}, bf16[72,1152]{1,0:T(8,128)(2,1)S(1)}, u32[]{:S(2)}) copy-start(bf16[72,1152]{1,0:T(8,128)(2,1)S(1)} %collective-permute-done.1.refs_7_) | copy-start | bytes 497668
  14.4 5.0 %collective-permute-start.2 = (bf16[72,1728]{1,0:T(8,128)(2,1)}, bf16[72,1728]{1,0:T(8,128)(2,1)S(1)}, u32[]{:S(2)}, u32[]{:S(2)}) collective-permute-start(bf16[72,1728]{1,0:T(8,128)(2,1)} %bitcast.13), channel_id=1, source_target_pairs={{0,1},{1,0},{2,3},{3,2},{4,5},{5,4},{6,7},{7,6},{8,9},{9,8},{10,11... | collective-permute-start | bytes 746504 | tf_op jit(solution)/shard_map/ppermute | solution.py:385
  18.8 1.8 %copy-start.1 = (f32[8,16,128]{2,1,0:T(8,128)}, f32[8,16,128]{2,1,0:T(8,128)S(1)}, u32[]{:S(2)}) copy-start(f32[8,16,128]{2,1,0:T(8,128)S(1)} %all-to-all-done.heard_ref) | copy-start | bytes 196612
  18.8 1.9 %copy-start.2 = (bf16[72,1728]{1,0:T(8,128)(2,1)}, bf16[72,1728]{1,0:T(8,128)(2,1)S(1)}, u32[]{:S(2)}) copy-start(bf16[72,1728]{1,0:T(8,128)(2,1)S(1)} %collective-permute-done.refs_3_) | copy-start | bytes 746500
  18.8 1.8 %collective-permute-start.3 = (bf16[72,1728]{1,0:T(8,128)(2,1)S(1)}, bf16[72,1728]{1,0:T(8,128)(2,1)S(1)}, u32[]{:S(2)}, u32[]{:S(2)}) collective-permute-start(bf16[72,1728]{1,0:T(8,128)(2,1)S(1)} %collective-permute-done.refs_3_), channel_id=1, source_target_pairs={{0,1},{1,0},{2,3},{3,2},{4,5},{5,4},{6,7},{7,6},{8,9},{9,8},{10,11... | collective-permute-start | bytes 746504 | tf_op jit(solution)/shard_map/ppermute | solution.py:405
  18.9 1.8 %copy-start.6 = (bf16[72,1152]{1,0:T(8,128)(2,1)}, bf16[72,1152]{1,0:T(8,128)(2,1)S(1)}, u32[]{:S(2)}) copy-start(bf16[72,1152]{1,0:T(8,128)(2,1)S(1)} %collective-permute-done.4.refs_8_) | copy-start | bytes 497668
  18.9 1.7 %collective-permute-start.5 = (bf16[72,1152]{1,0:T(8,128)(2,1)S(1)}, bf16[72,1152]{1,0:T(8,128)(2,1)S(1)}, u32[]{:S(2)}, u32[]{:S(2)}) collective-permute-start(bf16[72,1152]{1,0:T(8,128)(2,1)S(1)} %collective-permute-done.1.refs_7_), channel_id=1, source_target_pairs={{0,1},{1,0},{2,3},{3,2},{4,5},{5,4},{6,7},{7,6},{8,9},{9,8},{10,11... | collective-permute-start | bytes 497672 | tf_op jit(solution)/shard_map/ppermute | solution.py:405
  19.4 1.3 %copy-start.3 = (bf16[72,1728]{1,0:T(8,128)(2,1)}, bf16[72,1728]{1,0:T(8,128)(2,1)S(1)}, u32[]{:S(2)}) copy-start(bf16[72,1728]{1,0:T(8,128)(2,1)S(1)} %collective-permute-done.2.refs_4_) | copy-start | bytes 746500
  20.7 0.7 %copy-start.7 = (bf16[72,1152]{1,0:T(8,128)(2,1)}, bf16[72,1152]{1,0:T(8,128)(2,1)S(1)}, u32[]{:S(2)}) copy-start(bf16[72,1152]{1,0:T(8,128)(2,1)S(1)} %collective-permute-done.5.refs_9_) | copy-start | bytes 497668
  21.3 0.7 %copy-start.4 = (bf16[72,1728]{1,0:T(8,128)(2,1)}, bf16[72,1728]{1,0:T(8,128)(2,1)S(1)}, u32[]{:S(2)}) copy-start(bf16[72,1728]{1,0:T(8,128)(2,1)S(1)} %collective-permute-done.3.refs_5_) | copy-start | bytes 746500
  39.3 1.1 %copy-start = (bf16[576,1152]{1,0:T(8,128)(2,1)}, bf16[576,1152]{1,0:T(8,128)(2,1)S(1)}, u32[]{:S(2)}) copy-start(bf16[576,1152]{1,0:T(8,128)(2,1)S(1)} %collective-permute-done.7.refs_7_) | copy-start | bytes 3981316
  58.1 1.5 %collective-permute-start.8 = (f32[40,128]{1,0:T(8,128)}, f32[40,128]{1,0:T(8,128)S(1)}, u32[]{:S(2)}, u32[]{:S(2)}) collective-permute-start(f32[40,128]{1,0:T(8,128)} %shard_map.160.done_ref), channel_id=1, source_target_pairs={{0,1},{1,0},{2,3},{3,2},{4,5},{5,4},{6,7},{7,6},{8,9},{9,8},{10,11... | collective-permute-start | bytes 61448 | tf_op jit(solution)/shard_map/ppermute | solution.py:466
  59.6 0.6 copy-start.8

commit v3 on v2

--- a/solution.py
+++ b/solution.py
@@ -13,9 +13,10 @@
 LANES = 128
 ROWS = 8
 SUB = 16
-AHEAD = 2
+AHEAD = 3
 SLOTS = 4
 GRANT = 60 << 20
+GRANT_ALL = 66_400_000
 
 beta_low = 0.1
 beta_high = 20.0
@@ -104,7 +105,7 @@
         first = at % 2 * second
         target = stages[at] if stages else stack.at[pl.ds(first, own_rows), :]
         copies.append(pltpu.make_async_copy(source, target, sems.at[2 + at]))
-    for copy in copies:
+    for copy in copies[:2]:
         copy.start()
     count = heard_ref.shape[0]
     width = time_out_ref.shape[0]
@@ -128,6 +129,8 @@
     theirs = theirs & (at_row == at_lane - second + pair * own_rows)
     pick = jnp.where(mine | theirs, 1.0, 0.0).astype(bf16)
     copies[0].wait()
+    for copy in copies[2:]:
+        copy.start()
     hidden = silu(mm(features, time_in_ref[...])).astype(bf16)
     copies[1].wait()
     cond = silu(labels + mm(hidden, time_out_ref[...])).astype(bf16)
@@ -295,9 +298,11 @@
         stream[...] = mm(tok, patch8[...]) + pos_ref[...]
         inner[...] = (norm(stream[...]) * modv[index, 1:2, :] + modv[index, 0:1, :]).astype(bf16)
         fetched(index, 1)
+        fetched(index, 2)
+        fetched(index, 3)
+        fetched(index, 4)
         for kind in range(3):
             project(0, kind, qkv_own)
-        fetched(index, 2)
         for at in range(AHEAD):
             score(at)
         got = {}
@@ -316,8 +321,6 @@
                 pair = jnp.concatenate([got.pop(at - 1), got.pop(at)], axis=0)
                 first = (at - 1) * HEAD_DIM
                 mixed[first : first + 2 * HEAD_DIM, :] = pair.astype(bf16)
-        fetched(index, 3)
-        fetched(index, 4)
         turned[...] = mixed[...].T
         stream[...] += modv[index, 2:3, :] * mm(turned[...], out_all[...])
         inner[...] = (norm(stream[...]) * modv[index, 4:5, :] + modv[index, 3:4, :]).astype(bf16)
@@ -420,7 +423,7 @@
         + [pltpu.VMEM((2 * count, cols), f32)]
         + (like(near[2:]) if ada.shape[0] % ROWS else [])
         + [pltpu.SemaphoreType.DMA((len(near),))],
-        compiler_params=pltpu.CompilerParams(vmem_limit_bytes=GRANT),
+        compiler_params=pltpu.CompilerParams(vmem_limit_bytes=GRANT_ALL),
     )(heard, *near)
     mods = lax.all_to_all(parts, "dp", 0, 0, axis_index_groups=groups, tiled=True)
 
@@ -472,6 +475,7 @@
         ),
         in_specs=[VM, VM],
         out_specs=(VM, SM),
+        compiler_params=pltpu.CompilerParams(vmem_limit_bytes=GRANT_ALL),
     )(done, other)
 
 

time: 62 us -> 60.2 us (0.971)
  local copies, waits for them, and re-layouts: 3.03 us -> 1.29 us
    unnamed x18 -> x14, local copies, waits for them, and re-layouts: 3.03 us -> 1.29 us
where the time goes in v3:
time: 60.2 us; the launch traced here: 59.7 us
  Pallas kernels  25.2 us (42%)
  blocking collectives  12.4 us (21%)
  starting transfers between devices  10.5 us (17%)
  waiting for transfers between devices  9.53 us (16%)
  local copies, waits for them, and re-layouts  1.29 us (2%)
  between operations  0.72 us (1%)
    pallas_call x1, Pallas kernels, shards(): pl.pallas_call(step_kernel, out_shape=jax.ShapeDtypeStruct((lat_rows + RO...  17.5 us
    all_to_all x1, blocking collectives, shards(): lax.all_to_all(parts, 'dp', 0, 0, axis_index_groups=groups, tiled=True)  12.4 us
    all_to_all x1, starting transfers between devices, shards(): lax.all_to_all(told, 'dp', 0, 0, axis_index_groups=groups, tiled=True)  6.36 us
    pallas_call x1, Pallas kernels, shards(): pl.pallas_call(part_kernel, out_shape=jax.ShapeDtypeStruct((count, 2, col...  4.89 us
    all_to_all x1, waiting for transfers between devices, shards(): lax.all_to_all(told, 'dp', 0, 0, axis_index_groups=groups, tiled=True)  4.42 us
    ppermute x2, starting transfers between devices, shards(): ada_pair, fin_pair = (trade(ada), trade(final_ada))  2.93 us
    ppermute x2, waiting for transfers between devices, shards(): ada_pair, fin_pair = (trade(ada), trade(final_ada))  2.47 us
    pallas_call x1, Pallas kernels, shards(): pl.pallas_call(join_kernel, out_shape=(jax.ShapeDtypeStruct((2, latent),...  1.39 us
  transfers between devices with their start and end apart: 10, of which 4 were waited for; matrix products, arithmetic and copies ran while one was open for 0% of the time, Pallas kernels for 10%

profile of v3, /device:TPU:0, one launch (start us, length us, event | category | flops | bytes accessed | tf_op | source)
XLA Modules:
  0.0 59.7 jit_solution(1412711608539847934)
XLA Ops:
  0.6 0.6 collective-permute-start.6
  1.2 0.1 collective-permute-start.7
  1.3 2.9 %collective-permute-start = (bf16[72,1728]{1,0:T(8,128)(2,1)}, bf16[72,1728]{1,0:T(8,128)(2,1)S(1)}, u32[]{:S(2)}, u32[]{:S(2)}) collective-permute-start(bf16[72,1728]{1,0:T(8,128)(2,1)} %bitcast.12), channel_id=1, source_target_pairs={{0,2},{2,0},{4,6},{6,4},{8,10},{10,8},{12,14},{14,12},{16,18},{18,... | collective-permute-start | bytes 746504 | tf_op jit(solution)/shard_map/ppermute | solution.py:387
  4.2 0.0 collective-permute-start.1
  4.2 1.4 %shard_map.158 = f32[8,16,128]{2,1,0:T(8,128)} custom-call(f32[2]{0:T(128)} %time_hbm.3, f32[2]{0:T(128)} %step_hbm.3, bf16[2,1152]{1,0:T(2,128)(2,1)} %labels_hbm.1), custom_call_target="tpu_custom_call" | custom-call | tf_op jit(solution)/shard_map/pallas_call | solution.py:392
  5.6 6.4 %all-to-all-start = ((f32[8,16,128]{2,1,0:T(8,128)}), f32[8,16,128]{2,1,0:T(8,128)S(1)}, u32[]{:S(2)}, u32[]{:S(2)}) async-start(f32[8,16,128]{2,1,0:T(8,128)} %shard_map.158), calls=%async_computation | async-start | bytes 131072 | tf_op jit(solution)/shard_map/all_to_all | solution.py:406
  11.9 0.0 collective-permute-start.4
  11.9 2.5 %collective-permute-done.1.refs_7_ = bf16[72,1152]{1,0:T(8,128)(2,1)S(1)} collective-permute-done((bf16[72,1152]{1,0:T(8,128)(2,1)}, bf16[72,1152]{1,0:T(8,128)(2,1)S(1)}, u32[]{:S(2)}, u32[]{:S(2)}) %collective-permute-start.1) | collective-permute-done | bytes 165920 | tf_op jit(solution)/shard_map/ppermute | solution.py:387
  14.4 0.0 collective-permute-start.2
  14.4 4.4 %all-to-all-done.heard_ref = f32[8,16,128]{2,1,0:T(8,128)S(1)} async-done(((f32[8,16,128]{2,1,0:T(8,128)}), f32[8,16,128]{2,1,0:T(8,128)S(1)}, u32[]{:S(2)}, u32[]{:S(2)}) %all-to-all-start) | async-done | bytes 65568 | tf_op jit(solution)/shard_map/all_to_all | solution.py:406
  18.8 0.0 collective-permute-done.refs_3_
  18.8 0.1 collective-permute-start.3
  18.9 0.5 collective-permute-start.5
  19.4 0.0 collective-permute-done.2.refs_4_
  19.4 1.2 %collective-permute-done.5.refs_9_ = bf16[72,1152]{1,0:T(8,128)(2,1)S(1)} collective-permute-done((bf16[72,1152]{1,0:T(8,128)(2,1)S(1)}, bf16[72,1152]{1,0:T(8,128)(2,1)S(1)}, u32[]{:S(2)}, u32[]{:S(2)}) %collective-permute-start.5) | collective-permute-done | bytes 165920 | tf_op jit(solution)/shard_map/ppermute | solution.py:408
  20.7 0.7 %copy-done.5 = bf16[72,1152]{1,0:T(8,128)(2,1)} copy-done((bf16[72,1152]{1,0:T(8,128)(2,1)}, bf16[72,1152]{1,0:T(8,128)(2,1)S(1)}, u32[]{:S(2)}) %copy-start.5) | copy-done | bytes 165912
  21.3 0.0 collective-permute-done.3.refs_5_
  21.4 4.9 %shard_map.159 = bf16[8,2,5888]{2,1,0:T(2,128)(2,1)} custom-call(f32[8,16,128]{2,1,0:T(8,128)} %copy-done, bf16[256,1152]{1,0:T(8,128)(2,1)} %refs_0_.2, bf16[1152,1152]{1,0:T(8,128)(2,1)} %refs_1_.2, bf16[72,1728]{1,0:T(8,128)(2,1)} %bitcast.14, bf16[72,1728]{1,0:T(8,128)(2,1)} %copy-done.1, bf16[72,1728]{1,0:T(8,128)(2,1)} %copy-done.2, ...), custom_call_target="tpu_custom_call" | custom-call | tf_op jit(solution)/shard_map/pallas_call | solution.py:416
  26.3 12.4 %all_to_all.10.mods_ref = bf16[8,2,5888]{2,1,0:T(2,128)(2,1)} all-to-all(bf16[8,2,5888]{2,1,0:T(2,128)(2,1)} %shard_map.159), channel_id=1, replica_groups={{0,4,8,12,16,20,24,28},{2,6,10,14,18,22,26,30},{1,5,9,13,17,21,25,29},{..., dimensions={0} | all-to-all | bytes 376832 | tf_op jit(solution)/shard_map/all_to_all | solution.py:428
  38.7 17.5 %shard_map.160.done_ref = f32[40,128]{1,0:T(8,128)} custom-call(f32[2]{0:T(128)} %time_hbm.3, f32[2]{0:T(128)} %step_hbm.3, s32[2]{0:T(128)} %accept_hbm.1, bf16[8,2,5888]{2,1,0:T(2,128)(2,1)} %all_to_all.10.mods_ref, f32[2,4096]{1,0:T(2,128)} %refs_0_.3, f32[2,4096]{1,0:T(2,128)} %refs_1_.3, bf16[16,1152]{1,0:T(8,128)(2,1)} %refs_2_.1, ...), custom_call_target="tpu_custom_call" | custom-call | tf_op jit(solution)/shard_map/pallas_call | solution.py:437
  56.3 0.1 collective-permute-start.8
  56.3 1.4 %collective-permute-done.8.other_ref = f32[40,128]{1,0:T(8,128)S(1)} collective-permute-done((f32[40,128]{1,0:T(8,128)}, f32[40,128]{1,0:T(8,128)S(1)}, u32[]{:S(2)}, u32[]{:S(2)}) %collective-permute-start.8) | collective-permute-done | bytes 20512 | tf_op jit(solution)/shard_map/ppermute | solution.py:469
  57.7 0.6 %copy-done.6 = f32[40,128]{1,0:T(8,128)} copy-done((f32[40,128]{1,0:T(8,128)}, f32[40,128]{1,0:T(8,128)S(1)}, u32[]{:S(2)}) %copy-start.6) | copy-done | bytes 20504
  58.3 1.4 %shard_map.161 = (f32[2,4096]{1,0:T(2,128)}, f32[2]{0:T(128)}) custom-call(f32[40,128]{1,0:T(8,128)} %shard_map.160.done_ref, f32[40,128]{1,0:T(8,128)} %copy-done.6), custom_call_target="tpu_custom_call" | custom-call | tf_op jit(solution)/shard_map/pallas_call | solution.py:470
  (15 shorter events, 0.0 us)
Async XLA Ops:
  0.6 38.1 %collective-permute-start.6 = (bf16[3,576,1152]{2,1,0:T(8,128)(2,1)}, bf16[3,576,1152]{2,1,0:T(8,128)(2,1)}, u32[]{:S(2)}, u32[]{:S(2)}) collective-permute-start(bf16[3,576,1152]{2,1,0:T(8,128)(2,1)} %bitcast.8), channel_id=1, source_target_pairs={{0,1},{1,0},{2,3},{3,2},{4,5},{5,4},{6,7},{7,6},{8,9},{9,8},{10,11... | collective-permute-start | bytes 11943944 | tf_op jit(solution)/shard_map/ppermute | solution.py:389
  1.2 37.5 %collective-permute-start.7 = (bf16[576,1152]{1,0:T(8,128)(2,1)}, bf16[576,1152]{1,0:T(8,128)(2,1)}, u32[]{:S(2)}, u32[]{:S(2)}) collective-permute-start(bf16[576,1152]{1,0:T(8,128)(2,1)} %bitcast.10), channel_id=1, source_target_pairs={{0,1},{1,0},{2,3},{3,2},{4,5},{5,4},{6,7},{7,6},{8,9},{9,8},{10,11... | collective-permute-start | bytes 3981320 | tf_op jit(solution)/shard_map/ppermute | solution.py:389
  1.3 17.6 %collective-permute-start = (bf16[72,1728]{1,0:T(8,128)(2,1)}, bf16[72,1728]{1,0:T(8,128)(2,1)S(1)}, u32[]{:S(2)}, u32[]{:S(2)}) collective-permute-start(bf16[72,1728]{1,0:T(8,128)(2,1)} %bitcast.12), channel_id=1, source_target_pairs={{0,2},{2,0},{4,6},{6,4},{8,10},{10,8},{12,14},{14,12},{16,18},{18,... | collective-permute-start | bytes 746504 | tf_op jit(solution)/shard_map/ppermute | solution.py:387
  4.2 10.2 %collective-permute-start.1 = (bf16[72,1152]{1,0:T(8,128)(2,1)}, bf16[72,1152]{1,0:T(8,128)(2,1)S(1)}, u32[]{:S(2)}, u32[]{:S(2)}) collective-permute-start(bf16[72,1152]{1,0:T(8,128)(2,1)} %refs_6_.1), channel_id=1, source_target_pairs={{0,2},{2,0},{4,6},{6,4},{8,10},{10,8},{12,14},{14,12},{16,18},{18,... | collective-permute-start | bytes 497672 | tf_op jit(solution)/shard_map/ppermute | solution.py:387
  5.6 13.3 %all-to-all-start = ((f32[8,16,128]{2,1,0:T(8,128)}), f32[8,16,128]{2,1,0:T(8,128)S(1)}, u32[]{:S(2)}, u32[]{:S(2)}) async-start(f32[8,16,128]{2,1,0:T(8,128)} %shard_map.158), calls=%async_computation | async-start | bytes 131072 | tf_op jit(solution)/shard_map/all_to_all | solution.py:406
  11.9 7.0 %collective-permute-start.4 = (bf16[72,1152]{1,0:T(8,128)(2,1)}, bf16[72,1152]{1,0:T(8,128)(2,1)S(1)}, u32[]{:S(2)}, u32[]{:S(2)}) collective-permute-start(bf16[72,1152]{1,0:T(8,128)(2,1)} %refs_6_.1), channel_id=1, source_target_pairs={{0,1},{1,0},{2,3},{3,2},{4,5},{5,4},{6,7},{7,6},{8,9},{9,8},{10,11... | collective-permute-start | bytes 497672 | tf_op jit(solution)/shard_map/ppermute | solution.py:388
  14.4 5.0 %copy-start.3 = (bf16[72,1152]{1,0:T(8,128)(2,1)}, bf16[72,1152]{1,0:T(8,128)(2,1)S(1)}, u32[]{:S(2)}) copy-start(bf16[72,1152]{1,0:T(8,128)(2,1)S(1)} %collective-permute-done.1.refs_7_) | copy-start | bytes 497668
  14.4 5.0 %collective-permute-start.2 = (bf16[72,1728]{1,0:T(8,128)(2,1)}, bf16[72,1728]{1,0:T(8,128)(2,1)S(1)}, u32[]{:S(2)}, u32[]{:S(2)}) collective-permute-start(bf16[72,1728]{1,0:T(8,128)(2,1)} %bitcast.13), channel_id=1, source_target_pairs={{0,1},{1,0},{2,3},{3,2},{4,5},{5,4},{6,7},{7,6},{8,9},{9,8},{10,11... | collective-permute-start | bytes 746504 | tf_op jit(solution)/shard_map/ppermute | solution.py:388
  18.8 2.5 %copy-start = (f32[8,16,128]{2,1,0:T(8,128)}, f32[8,16,128]{2,1,0:T(8,128)S(1)}, u32[]{:S(2)}) copy-start(f32[8,16,128]{2,1,0:T(8,128)S(1)} %all-to-all-done.heard_ref) | copy-start | bytes 196612
  18.8 2.5 %copy-start.1 = (bf16[72,1728]{1,0:T(8,128)(2,1)}, bf16[72,1728]{1,0:T(8,128)(2,1)S(1)}, u32[]{:S(2)}) copy-start(bf16[72,1728]{1,0:T(8,128)(2,1)S(1)} %collective-permute-done.refs_3_) | copy-start | bytes 746500
  18.8 2.5 %collective-permute-start.3 = (bf16[72,1728]{1,0:T(8,128)(2,1)S(1)}, bf16[72,1728]{1,0:T(8,128)(2,1)}, u32[]{:S(2)}, u32[]{:S(2)}) collective-permute-start(bf16[72,1728]{1,0:T(8,128)(2,1)S(1)} %collective-permute-done.refs_3_), channel_id=1, source_target_pairs={{0,1},{1,0},{2,3},{3,2},{4,5},{5,4},{6,7},{7,6},{8,9},{9,8},{10,11... | collective-permute-start | bytes 746504 | tf_op jit(solution)/shard_map/ppermute | solution.py:408
  18.9 1.7 %copy-start.4 = (bf16[72,1152]{1,0:T(8,128)(2,1)}, bf16[72,1152]{1,0:T(8,128)(2,1)S(1)}, u32[]{:S(2)}) copy-start(bf16[72,1152]{1,0:T(8,128)(2,1)S(1)} %collective-permute-done.4.refs_8_) | copy-start | bytes 497668
  18.9 1.7 %collective-permute-start.5 = (bf16[72,1152]{1,0:T(8,128)(2,1)S(1)}, bf16[72,1152]{1,0:T(8,128)(2,1)S(1)}, u32[]{:S(2)}, u32[]{:S(2)}) collective-permute-start(bf16[72,1152]{1,0:T(8,128)(2,1)S(1)} %collective-permute-done.1.refs_7_), channel_id=1, source_target_pairs={{0,1},{1,0},{2,3},{3,2},{4,5},{5,4},{6,7},{7,6},{8,9},{9,8},{10,11... | collective-permute-start | bytes 497672 | tf_op jit(solution)/shard_map/ppermute | solution.py:408
  19.4 1.9 %copy-start.2 = (bf16[72,1728]{1,0:T(8,128)(2,1)}, bf16[72,1728]{1,0:T(8,128)(2,1)S(1)}, u32[]{:S(2)}) copy-start(bf16[72,1728]{1,0:T(8,128)(2,1)S(1)} %collective-permute-done.2.refs_4_) | copy-start | bytes 746500
  20.7 0.7 %copy-start.5 = (bf16[72,1152]{1,0:T(8,128)(2,1)}, bf16[72,1152]{1,0:T(8,128)(2,1)S(1)}, u32[]{:S(2)}) copy-start(bf16[72,1152]{1,0:T(8,128)(2,1)S(1)} %collective-permute-done.5.refs_9_) | copy-start | bytes 497668
  56.3 1.5 %collective-permute-start.8 = (f32[40,128]{1,0:T(8,128)}, f32[40,128]{1,0:T(8,128)S(1)}, u32[]{:S(2)}, u32[]{:S(2)}) collective-permute-start(f32[40,128]{1,0:T(8,128)} %shard_map.160.done_ref), channel_id=1, source_target_pairs={{0,1},{1,0},{2,3},{3,2},{4,5},{5,4},{6,7},{7,6},{8,9},{9,8},{10,11... | collective-permute-start | bytes 61448 | tf_op jit(solution)/shard_map/ppermute | solution.py:469
  57.7 0.6 %copy-start.6 = (f32[40,128]{1,0:T(8,128)}, f32[40,128]{1,0:T(8,128)S(1)}, u32[]{:S(2)}) copy-start(f32[40,128]{1,0:T(8,128)S(1)} %collective-permute-done.8.other_ref) | copy-start | bytes 61444
